TPU v7x, 128 devices: a whole 4x4x4 slice. The times are simulated.
128 devices in a mesh: rows: 64 (over x, y_hi, z, core), grp: 2 (over y_lo).
Axes of the slice: x: 4, y: 4 (y_hi: 2, y_lo: 2; y = y_hi * 2 + y_lo), z: 4, core: 2. Of those that a mesh axis runs over, the one named last changes fastest.
Arguments:
- snapshots: float32 [524288, 256], P(('rows', 'grp'))
- blocks: bfloat16 [4096, 16, 128, 128], P(('rows', 'grp')), may hold values from -96 to 96
- columns: int32 [4096, 16], P(('rows', 'grp')), may hold values from 0 to 63
Outputs:
- projected: float32 [256, 256], replicated
- scaled_factor: float32 [256, 256], replicated
Inputs may be any that keep to these rules, and one draw needn't show every extreme that they name: `columns`: each stored block couples its block row to a block row of the same group of 2 * 32 consecutive block rows.
All inputs are finite; a program needn't handle non-finite values.
Results may differ from a plain program's by a relative error of at most 0.003.
Values may be sent and summed in bfloat16 or wider, within the bound.
No kernel may reach another device: no remote copies, remote signals or barrier semaphores. Data moves between devices by JAX's collectives and lax.ppermute only.
A program may use at most 192 MiB of HBM per device.

v0:
```python
import math

import jax
import jax.numpy as jnp
from jax import lax
from jax.sharding import PartitionSpec as P


def from_partner(value, axis, stride):
    mask = 2**stride
    pairs = [(source, source ^ mask) for source in range(lax.axis_size(axis))]
    return lax.ppermute(value, axis, pairs)


def inner_gram(left, right):
    return lax.dot_general(
        left,
        right,
        (((0,), (0,)), ((), ())),
        precision=lax.Precision.HIGHEST,
        preferred_element_type=jnp.float32,
    )


def upper_inverse(factor):
    size = factor.shape[0]
    unit_rows = jnp.eye(size, dtype=factor.dtype)

    def substitute(count, inverse):
        index = (size - 1 - count).astype(jnp.int32)
        frow = lax.dynamic_slice_in_dim(factor, index, 1, 0)
        unit = lax.dynamic_slice_in_dim(unit_rows, index, 1, 0)
        pivot = lax.dynamic_slice(factor, (index, index), (1, 1))
        fresh = (unit - jnp.dot(frow, inverse, precision=lax.Precision.HIGHEST)) / pivot
        return lax.dynamic_update_slice_in_dim(inverse, fresh, index, 0)

    return lax.fori_loop(jnp.int32(0), jnp.int32(size), substitute, jnp.zeros_like(factor))


def local(snapshots, blocks, columns):
    local_gram = inner_gram(snapshots, snapshots)
    factor = jnp.linalg.cholesky(local_gram).T
    levels = lax.axis_size(("rows", "grp")).bit_length() - 1
    for bit in range(levels):
        partner = from_partner(factor, ("rows", "grp"), bit)
        combined = inner_gram(factor, factor) + inner_gram(partner, partner)
        factor = jnp.linalg.cholesky(combined).T
    inverse = upper_inverse(factor)
    basis = jnp.dot(snapshots, inverse, precision=lax.Precision.HIGHEST)
    basis_half = basis.astype(jnp.bfloat16)
    block_len = blocks.shape[2]
    width = snapshots.shape[1]
    gathered = lax.all_gather(basis_half, "grp", axis=0, tiled=True)
    window = gathered.reshape(gathered.shape[0] // block_len, block_len, width)
    picked = jnp.take(window, columns, axis=0)
    image = jnp.einsum("bjrc,bjck->brk", blocks, picked, preferred_element_type=jnp.float32)
    image = image.reshape(snapshots.shape[0], width)
    partial_terms = inner_gram(basis, image)
    projected = lax.psum(partial_terms, ("rows", "grp"))
    total_rows = snapshots.shape[0] * lax.axis_size(("rows", "grp"))
    scaled_factor = factor / math.sqrt(total_rows)
    return (projected, scaled_factor)


def solution(mesh):
    return jax.shard_map(
        local,
        mesh=mesh,
        in_specs=(
            P(("rows", "grp"), None),
            P(("rows", "grp"), None, None, None),
            P(("rows", "grp"), None),
        ),
        out_specs=(P(), P()),
        check_vma=False,
    )
```

profile of v0, /device:TPU:1, one launch (start us, length us, event | category | flops | bytes accessed | tf_op | source)
XLA Modules:
  0.0 1051.0 jit_solution(15019776480115702252)
XLA Ops:
  7.2 10.1 fusion.133
  17.5 11.7 %cholesky.382 = f32[128,128]{1,0:T(8,128)S(1)} custom-call(f32[128,128]{1,0:T(8,128)S(1)} %cholesky.650), custom_call_target="Cholesky" | custom-call | tf_op jit(solution)/shard_map/jit(cholesky)/cholesky | solution.py:42
  29.2 9.8 custom-call.15
  39.5 11.7 %cholesky.399 = f32[128,128]{1,0:T(8,128)S(1)} custom-call(f32[128,128]{1,0:T(8,128)S(1)} %convolution_subtract_fusion.1), custom_call_target="Cholesky" | custom-call | tf_op jit(solution)/shard_map/jit(cholesky)/cholesky | solution.py:42
  63.0 11.7 %cholesky.416 = f32[128,128]{1,0:T(8,128)S(1)} custom-call(f32[128,128]{1,0:T(8,128)S(1)} %cholesky.653), custom_call_target="Cholesky" | custom-call | tf_op jit(solution)/shard_map/jit(cholesky)/cholesky | solution.py:47
  86.4 11.7 %cholesky.433 = f32[128,128]{1,0:T(8,128)S(1)} custom-call(f32[128,128]{1,0:T(8,128)S(1)} %slice_subtract_fusion.6), custom_call_target="Cholesky" | custom-call | tf_op jit(solution)/shard_map/jit(cholesky)/cholesky | solution.py:47
  106.6 11.7 %cholesky.450 = f32[128,128]{1,0:T(8,128)S(1)} custom-call(f32[128,128]{1,0:T(8,128)S(1)} %cholesky.656), custom_call_target="Cholesky" | custom-call | tf_op jit(solution)/shard_map/jit(cholesky)/cholesky | solution.py:47
  130.0 11.7 %cholesky.467 = f32[128,128]{1,0:T(8,128)S(1)} custom-call(f32[128,128]{1,0:T(8,128)S(1)} %slice_subtract_fusion.5), custom_call_target="Cholesky" | custom-call | tf_op jit(solution)/shard_map/jit(cholesky)/cholesky | solution.py:47
  155.4 11.7 %cholesky.484 = f32[128,128]{1,0:T(8,128)S(1)} custom-call(f32[128,128]{1,0:T(8,128)S(1)} %cholesky.659), custom_call_target="Cholesky" | custom-call | tf_op jit(solution)/shard_map/jit(cholesky)/cholesky | solution.py:47
  178.7 11.7 %cholesky.501 = f32[128,128]{1,0:T(8,128)S(1)} custom-call(f32[128,128]{1,0:T(8,128)S(1)} %slice_subtract_fusion.4), custom_call_target="Cholesky" | custom-call | tf_op jit(solution)/shard_map/jit(cholesky)/cholesky | solution.py:47
  204.7 11.7 %cholesky.518 = f32[128,128]{1,0:T(8,128)S(1)} custom-call(f32[128,128]{1,0:T(8,128)S(1)} %cholesky.662), custom_call_target="Cholesky" | custom-call | tf_op jit(solution)/shard_map/jit(cholesky)/cholesky | solution.py:47
  228.1 11.7 %cholesky.535 = f32[128,128]{1,0:T(8,128)S(1)} custom-call(f32[128,128]{1,0:T(8,128)S(1)} %slice_subtract_fusion.3), custom_call_target="Cholesky" | custom-call | tf_op jit(solution)/shard_map/jit(cholesky)/cholesky | solution.py:47
  253.1 11.7 %cholesky.552 = f32[128,128]{1,0:T(8,128)S(1)} custom-call(f32[128,128]{1,0:T(8,128)S(1)} %cholesky.665), custom_call_target="Cholesky" | custom-call | tf_op jit(solution)/shard_map/jit(cholesky)/cholesky | solution.py:47
  276.5 11.7 %cholesky.569 = f32[128,128]{1,0:T(8,128)S(1)} custom-call(f32[128,128]{1,0:T(8,128)S(1)} %slice_subtract_fusion.2), custom_call_target="Cholesky" | custom-call | tf_op jit(solution)/shard_map/jit(cholesky)/cholesky | solution.py:47
  298.6 11.7 %cholesky.586 = f32[128,128]{1,0:T(8,128)S(1)} custom-call(f32[128,128]{1,0:T(8,128)S(1)} %cholesky.668), custom_call_target="Cholesky" | custom-call | tf_op jit(solution)/shard_map/jit(cholesky)/cholesky | solution.py:47
  322.0 11.7 %cholesky.603 = f32[128,128]{1,0:T(8,128)S(1)} custom-call(f32[128,128]{1,0:T(8,128)S(1)} %slice_subtract_fusion.1), custom_call_target="Cholesky" | custom-call | tf_op jit(solution)/shard_map/jit(cholesky)/cholesky | solution.py:47
  345.7 11.7 %cholesky.620 = f32[128,128]{1,0:T(8,128)S(1)} custom-call(f32[128,128]{1,0:T(8,128)S(1)} %cholesky.671), custom_call_target="Cholesky" | custom-call | tf_op jit(solution)/shard_map/jit(cholesky)/cholesky | solution.py:47
  357.5 9.8 custom-call.22
  367.8 11.7 %cholesky.637 = f32[128,128]{1,0:T(8,128)S(1)} custom-call(f32[128,128]{1,0:T(8,128)S(1)} %slice_subtract_fusion), custom_call_target="Cholesky" | custom-call | tf_op jit(solution)/shard_map/jit(cholesky)/cholesky | solution.py:47
  382.4 388.4 %while.12 = (s32[]{:T(128)}, f32[256,256]{1,0:T(8,128)S(1)}, f32[256,256]{1,0:T(8,128)S(1)}, f32[256,256]{1,0:T(8,128)S(1)}, s32[]{:T(128)}, /*index=5*/s32[]{:T(128)}, s32[]{:T(128)}, s32[]{:T(128)}) while((s32[]{:T(128)}, f32[256,256]{1,0:T(8,128)S(1)}, f32[256,256]{1,0:T(8,128)S(1)}, f32[256,256]{1,0:T(8,128)S(1)}, s32[]{:T(128)}, ...), condition=%wide.region_5.7_spmd, body=%wide.region_4.6_spmd.sunk | while | flops 786950 | bytes 268439 | solution.py:37
  783.5 64.5 %all-gather.2.cloned.1.call-done = bf16[8192,256]{0,1:T(8,128)(2,1)} async-done(((bf16[4096,256]{0,1:T(8,128)(2,1)}), bf16[8192,256]{0,1:T(8,128)(2,1)}) %all-gather.2.cloned.1.call-update) | async-done | bytes 4194320 | tf_op jit(solution)/shard_map/all_gather | solution.py:53
  854.3 18.3 %gather_fusion = bf16[512,128,256]{2,1,0:T(8,128)(2,1)} fusion(bf16[64,128,256]{2,1,0:T(8,128)(2,1)} %bitcast.165, s32[1024]{0:T(1024)S(1)} %pad_clamp_fusion), kind=kCustom, calls=%fused_computation | custom fusion | bytes 67110912 | tf_op jit(solution)/shard_map/jit(_take)/gather | solution.py:55
  872.6 20.2 %fusion.4 = f32[32,256,128,1]{1,2,3,0:T(8,128)} fusion(bf16[32,16,128,128]{3,2,1,0:T(8,128)(2,1)} %param.7, bf16[32,16,128,256]{3,2,1,0:T(8,128)(2,1)} %bitcast.166, pred[32,16]{1,0:T(8,128)(4,1)S(1)} %copy.54), kind=kOutput, calls=%fused_computation.6 | convolution fusion | flops 4311744512 | bytes 54526464 | tf_op jit(solution)/shard_map/bjrc,bjck->brk/dot_general | solution.py:56
  900.3 141.8 %all-reduce.3.cloned.1.call-done = f32[256,256]{1,0:T(8,128)} async-done(((f32[256,256]{1,0:T(8,128)}), f32[256,256]{1,0:T(8,128)}) %all-reduce.3.cloned.1.call-update) | async-done | bytes 262160 | tf_op jit(solution)/shard_map/psum | solution.py:59
  (916 shorter events, 556.0 us)
Async XLA Ops:
  7.2 840.8 %all-gather.2.cloned.1.call-start = ((), (), s32[]{:S(2)}) async-start(), calls=%async_computation | async-start | bytes 6291456 | tf_op jit(solution)/shard_map/all_gather | solution.py:53
  51.3 2.1 copy-start.2
  54.4 8.0 collective-permute-start
  102.4 3.6 collective-permute-start.1
  146.1 8.7 collective-permute-start.2
  194.8 9.3 collective-permute-start.3
  244.1 8.4 collective-permute-start.4
  292.5 5.5 collective-permute-start.5
  338.0 7.0 collective-permute-start.6
  779.4 2.0 copy-start
  781.5 1.7 copy-start.3
  783.1 259.0 %all-reduce.3.cloned.1.call-start = ((), (), s32[]{:S(2)}) async-start(), calls=%async_computation.1 | async-start | bytes 524288 | tf_op jit(solution)/shard_map/psum | solution.py:59
  872.6 20.2 %copy-start.1 = (f32[256,4096]{1,0:T(8,128)S(1)}, f32[256,4096]{1,0:T(8,128)}, u32[]{:S(2)}) copy-start(f32[256,4096]{1,0:T(8,128)} %copy-done) | copy-start | bytes 12582916
Sparse Core Ops, SparseCore 0:
  783.2 64.6 all-gather.1
  899.5 142.5 all-reduce.2
where the time goes:
time: 1070 us; the launch traced here: 1050 us
  other arithmetic  289 us (27%)
  matrix products  279 us (26%)
  waiting for transfers between devices  229 us (21%)
  local copies, waits for them, and re-layouts  203 us (19%)
  between operations  25.8 us (2%)
  starting transfers between devices  18.1 us (2%)
    another operation x49, other arithmetic, local(): factor = jnp.linalg.cholesky(combined).T  246 us
    dot_general x256, matrix products, substitute(): jnp.dot(frow, inverse, precision=lax.Precision.HIGHEST)  213 us
    dynamic_slice x256, local copies, waits for them, and re-layouts, substitute(): pivot = lax.dynamic_slice(factor, (index, index), (1, 1))  152 us
    psum x1, waiting for transfers between devices, local(): projected = lax.psum(partial_terms, ('rows', 'grp'))  142 us
    all_gather x1, waiting for transfers between devices, local(): gathered = lax.all_gather(basis_half, 'grp', axis=0, tiled=True)  64.5 us
    another operation x6, other arithmetic, local(): factor = jnp.linalg.cholesky(local_gram).T  34 us
    dot_general x16, matrix products, inner_gram(): lax.dot_general(left, right, (((0,), (0,)), ((), ())), precision=lax.Prec...  29.6 us
    ppermute x7, waiting for transfers between devices, from_partner(): return lax.ppermute(value, axis, pairs)  22.3 us
  transfers between devices with their start and end apart: 9, of which 8 were waited for; matrix products, arithmetic and copies ran while one was open for 1% of the time, Pallas kernels for 0%

commit v1 on v0

v1 whole, which is shorter than its diff:
```python
import functools
import math

import jax
import jax.numpy as jnp
from jax import lax
from jax.experimental import pallas as pl
from jax.experimental.pallas import tpu as pltpu
from jax.sharding import PartitionSpec as P

HIGHEST = lax.Precision.HIGHEST
AXES = ("x", "yh", "z", "core", "yl")
SIDE = ("x", "z", "core")
PANEL = 64
FIRST = 8
RAW = 16
KEPT = 8
ROW_TILE = 512
PAIR = 2
LIGHT = pl.CostEstimate(flops=0, transcendentals=0, bytes_accessed=0)
EARLY_VMEM = 40 << 20
LATE_VMEM = 40 << 20


def tdot(left, right):
    return lax.dot_general(left, right, (((0,), (0,)), ((), ())), preferred_element_type=jnp.float32)


def thirds(value):
    high = value.astype(jnp.bfloat16)
    rest = value - high.astype(jnp.float32)
    mid = rest.astype(jnp.bfloat16)
    low = (rest - mid.astype(jnp.float32)).astype(jnp.bfloat16)
    return high, mid, low


def gram_kernel(x_ref, g_ref, sym_ref, off_ref):
    step = pl.program_id(0)

    @pl.when(step == 0)
    def _():
        sym_ref[...] = jnp.zeros_like(sym_ref)
        off_ref[...] = jnp.zeros_like(off_ref)

    high, mid, low = thirds(x_ref[...])
    both = jnp.concatenate([high, mid], axis=0)
    sym_ref[...] += tdot(both, both)
    off_ref[...] += tdot(jnp.concatenate([high, high], axis=0), jnp.concatenate([mid, low], axis=0))

    @pl.when(step == pl.num_programs(0) - 1)
    def _():
        off = off_ref[...]
        g_ref[...] = sym_ref[...] + (off + off.T)


def local_gram(snapshots):
    rows, width = snapshots.shape
    return pl.pallas_call(
        gram_kernel,
        grid=(rows // ROW_TILE,),
        in_specs=[pl.BlockSpec((ROW_TILE, width), lambda i: (i, 0))],
        out_specs=pl.BlockSpec((width, width), lambda i: (0, 0)),
        out_shape=jax.ShapeDtypeStruct((width, width), jnp.float32),
        scratch_shapes=[pltpu.VMEM((width, width), jnp.float32)] * 2,
        cost_estimate=LIGHT,
        name="local_gram",
    )(snapshots)


def factor_kernel(scale, g_ref, sf_ref, inv_ref, r_ref, l_ref):
    n = g_ref.shape[0]
    sub = lax.broadcasted_iota(jnp.int32, (8, 128), 0)
    lane = lax.broadcasted_iota(jnp.int32, (8, 128), 1)
    r_ref[...] = jnp.zeros_like(r_ref)
    l_ref[...] = jnp.zeros_like(l_ref)
    for r0 in range(0, n, PANEL):
        first = r0 // 128
        keys = [("r", i) for i in range(first, n // 128)] + [("l", i) for i in range(first + 1)]
        depth = -(-r0 // 128) * 128
        left = None
        if depth:
            a = first * 128
            left = r_ref[0:depth, a:a + 128].T[r0 - a:r0 - a + PANEL, :]
        tile = {}
        for key in keys:
            kind, i = key
            if kind == "r":
                part = g_ref[r0:r0 + PANEL, i * 128:(i + 1) * 128]
            else:
                rows = lax.broadcasted_iota(jnp.int32, (PANEL, 128), 0) + r0
                cols = lax.broadcasted_iota(jnp.int32, (PANEL, 128), 1) + i * 128
                part = jnp.where(rows == cols, 1.0, 0.0).astype(jnp.float32)
            if depth:
                right = (r_ref if kind == "r" else l_ref)[0:depth, i * 128:(i + 1) * 128]
                part = part - jnp.dot(left, right, precision=HIGHEST, preferred_element_type=jnp.float32)
            for t in range(PANEL // 8):
                tile[t, key] = part[t * 8:(t + 1) * 8, :]
        pk = ("r", first)
        nt = PANEL // 8
        for tk in range(nt):
            c0 = (r0 + tk * 8) % 128
            cols = {}
            for q in range(8):
                for t in range(tk, nt):
                    cols[t, q] = jnp.broadcast_to(tile[t, pk][:, c0 + q:c0 + q + 1], (8, 128))
            rows = {}
            for q in range(8):
                pivot = jnp.broadcast_to(cols[tk, q][q:q + 1, :], (8, 128))
                recip = 1.0 / pivot
                for key in keys:
                    rows[q, key] = jnp.broadcast_to(tile[tk, key][q:q + 1, :], (8, 128)) * recip
                below = jnp.where(sub > q, cols[tk, q], 0.0)
                if q < 7:
                    for key in keys:
                        tile[tk, key] = tile[tk, key] - below * rows[q, key]
                for p in range(q + 1, 8):
                    coef = jnp.broadcast_to(cols[tk, p][q:q + 1, :], (8, 128)) * recip
                    cols[tk, p] = cols[tk, p] - below * coef
                    for t in range(tk + 1, nt):
                        cols[t, p] = cols[t, p] - cols[t, q] * coef
            for t in range(tk + 1, nt):
                for key in keys:
                    acc = tile[t, key]
                    for q in range(8):
                        acc = acc - cols[t, q] * rows[q, key]
                    tile[t, key] = acc
        for t in range(nt):
            at = sub + (r0 + t * 8 - first * 128)
            diag = jnp.sum(jnp.where(lane == at, tile[t, pk], 0.0), axis=1, keepdims=True)
            scale_rows = jnp.broadcast_to(1.0 / jnp.sqrt(diag), (8, 128))
            for key in keys:
                value = tile[t, key] * scale_rows
                if key == pk:
                    value = jnp.where(lane >= at, value, 0.0)
                (r_ref if key[0] == "r" else l_ref)[r0 + t * 8:r0 + t * 8 + 8, key[1] * 128:(key[1] + 1) * 128] = value
    sf_ref[...] = r_ref[...] * scale
    high, mid, low = thirds(l_ref[...].T)
    for at, part in enumerate([high, mid, low, high, mid, high]):
        inv_ref[at * n:(at + 1) * n, :] = part

def factorize(gram, scale):
    size = gram.shape[0]
    return pl.pallas_call(
        functools.partial(factor_kernel, scale),
        out_shape=[
            jax.ShapeDtypeStruct((size, size), jnp.float32),
            jax.ShapeDtypeStruct((6 * size, size), jnp.bfloat16),
        ],
        in_specs=[pl.BlockSpec(memory_space=pltpu.VMEM)],
        out_specs=[pl.BlockSpec(memory_space=pltpu.VMEM)] * 2,
        scratch_shapes=[pltpu.VMEM((size, size), jnp.float32)] * 2,
        cost_estimate=LIGHT,
        name="factorize",
    )(gram)


def basis_of(value, inverse):
    high, mid, low = thirds(value)
    terms = jnp.concatenate([low, mid, high, mid, high, high], axis=1)
    basis = jnp.dot(terms, inverse, preferred_element_type=jnp.float32)
    half = basis.astype(jnp.bfloat16)
    return half, (basis - half.astype(jnp.float32)).astype(jnp.bfloat16)


def late_basis_kernel(x_ref, inv_ref, send_ref, half_ref, low_ref):
    half, low = basis_of(x_ref[...], inv_ref[...])
    send_ref[...] = half
    half_ref[...] = half
    low_ref[...] = low


def late_basis(snapshots, inverse, start):
    rows, width = snapshots.shape
    first = start // ROW_TILE
    shifted = pl.BlockSpec((ROW_TILE, width), lambda i: (i + first, 0))
    half = jax.ShapeDtypeStruct((rows, width), jnp.bfloat16)
    return pl.pallas_call(
        late_basis_kernel,
        grid=((rows - start) // ROW_TILE,),
        in_specs=[shifted, pl.BlockSpec(inverse.shape, lambda i: (0, 0))],
        out_specs=[pl.BlockSpec((ROW_TILE, width), lambda i: (i, 0)), shifted, shifted],
        out_shape=[jax.ShapeDtypeStruct((rows - start, width), jnp.bfloat16), half, half],
        cost_estimate=LIGHT,
        name="late_basis",
    )(snapshots, inverse)


def early_basis_kernel(ends, x_ref, one_ref, two_ref, inv_ref, _, __, half_ref, low_ref, other_ref):
    step = pl.program_id(0)
    value = jnp.where(step < ends[0], x_ref[...], jnp.where(step < ends[1], one_ref[...], two_ref[...]))
    half, low = basis_of(value, inv_ref[...])

    @pl.when(step < ends[0])
    def _():
        half_ref[...] = half
        low_ref[...] = low

    @pl.when(step >= ends[0])
    def _():
        other_ref[...] = half


def early_basis(snapshots, one, two, inverse, half, low):
    width = snapshots.shape[1]
    own = (one.shape[0] + two.shape[0]) // ROW_TILE
    mid = own + one.shape[0] // ROW_TILE
    spec = lambda index: pl.BlockSpec((ROW_TILE, width), index)
    here = spec(lambda i: (jnp.minimum(i, own - 1), 0))
    return pl.pallas_call(
        functools.partial(early_basis_kernel, (own, mid)),
        grid=(2 * own,),
        in_specs=[
            here,
            spec(lambda i: (jnp.clip(i - own, 0, mid - own - 1), 0)),
            spec(lambda i: (jnp.maximum(i - mid, 0), 0)),
            pl.BlockSpec(inverse.shape, lambda i: (0, 0)),
            pl.BlockSpec(memory_space=pl.ANY),
            pl.BlockSpec(memory_space=pl.ANY),
        ],
        out_specs=[here, here, spec(lambda i: (jnp.maximum(i - own, 0), 0))],
        out_shape=[
            jax.ShapeDtypeStruct(half.shape, half.dtype),
            jax.ShapeDtypeStruct(low.shape, low.dtype),
            jax.ShapeDtypeStruct((own * ROW_TILE, width), half.dtype),
        ],
        input_output_aliases={4: 0, 5: 1},
        cost_estimate=LIGHT,
        name="early_basis",
    )(snapshots, one, two, inverse, half, low)


def load_window(step, out_ref, window_ref, sems, pieces, places):
    @pl.when(step == 0)
    def _():
        copies = [
            pltpu.make_async_copy(piece, window_ref.at[pl.ds(at, piece.shape[0])], sems.at[i])
            for i, (piece, at) in enumerate(zip(pieces, places))
        ]
        for copy in copies:
            copy.start()
        out_ref[...] = jnp.zeros_like(out_ref)
        window_ref[window_ref.shape[0] - 1] = jnp.zeros(window_ref.shape[1:], window_ref.dtype)
        for copy in copies:
            copy.wait()


def row_image(block, spot, stored, window_ref):
    image = jnp.zeros(window_ref.shape[1:], jnp.float32)
    for j in range(0, stored, 2):
        left = jnp.concatenate([block(j), block(j + 1)], axis=1)
        right = jnp.concatenate([window_ref[spot(j)], window_ref[spot(j + 1)]], axis=0)
        image += jnp.dot(left, right, preferred_element_type=jnp.float32)
    return image


def add_terms(out_ref, half, low, image):
    high = image.astype(jnp.bfloat16)
    rest = (image - high.astype(jnp.float32)).astype(jnp.bfloat16)
    width = image.shape[1]
    pair = tdot(half, jnp.concatenate([high, rest], axis=1))
    out_ref[...] += pair[:, :width] + (pair[:, width:] + tdot(low, high))


def early_kernel(places, spot_ref, late_ref, blocks_ref, half_ref, low_ref, *refs):
    pieces, (out_ref, kept_ref, window_ref, sems) = refs[:-4], refs[-4:]
    step = pl.program_id(0)
    load_window(step, out_ref, window_ref, sems, pieces, places)
    images = []
    for row in range(PAIR):
        at = step * PAIR + row
        images.append(
            row_image(lambda j: blocks_ref[row, j], lambda j: spot_ref[at, j], blocks_ref.shape[1], window_ref)
        )
        for r in range(kept_ref.shape[1]):
            kept_ref[row, r] = blocks_ref[row, late_ref[at, r]]
    add_terms(out_ref, half_ref[...], low_ref[...], jnp.concatenate(images, axis=0))


def late_kernel(places, spot_ref, late_ref, fill_ref, kept_ref, half_ref, low_ref, blocks_ref, *refs):
    pieces, (out_ref, window_ref, block_ref, sems, block_sem) = refs[:-5], refs[-5:]
    step = pl.program_id(0)
    load_window(step, out_ref, window_ref, sems, pieces, places)
    size = window_ref.shape[1]
    kept = kept_ref.shape[1]
    images = []
    for row in range(PAIR):
        at = step * PAIR + row
        images.append(
            row_image(lambda j: kept_ref[row, j], lambda j: spot_ref[at, j], kept, window_ref)
        )
    add_terms(out_ref, half_ref[...], low_ref[...], jnp.concatenate(images, axis=0))
    for row in range(PAIR):
        at = step * PAIR + row

        @pl.when(fill_ref[at] > kept)
        def _():
            def more(r, image):
                copy = pltpu.make_async_copy(blocks_ref.at[at, late_ref[at, r]], block_ref, block_sem)
                copy.start()
                copy.wait()
                return image + jnp.dot(
                    block_ref[...], window_ref[spot_ref[at, r]], preferred_element_type=jnp.float32
                )

            zero = jnp.zeros(window_ref.shape[1:], jnp.float32)
            image = lax.fori_loop(kept, fill_ref[at], more, zero)
            span = slice(row * size, (row + 1) * size)
            add_terms(out_ref, half_ref[span, :], low_ref[span, :], image)


def as_blocks(pieces, size):
    return [piece.reshape(piece.shape[0] // size, size, piece.shape[1]) for piece in pieces]


def early_terms(spots, late, blocks, half, low, pieces, places, slots):
    count, stored, size, _ = blocks.shape
    width = half.shape[1]
    return pl.pallas_call(
        functools.partial(early_kernel, places),
        grid_spec=pltpu.PrefetchScalarGridSpec(
            num_scalar_prefetch=2,
            grid=(count // PAIR,),
            in_specs=[
                pl.BlockSpec((PAIR, stored, size, size), lambda i, *_: (i, 0, 0, 0)),
                pl.BlockSpec((PAIR * size, width), lambda i, *_: (i, 0)),
                pl.BlockSpec((PAIR * size, width), lambda i, *_: (i, 0)),
            ]
            + [pl.BlockSpec(memory_space=pl.ANY)] * len(pieces),
            out_specs=[
                pl.BlockSpec((width, width), lambda i, *_: (0, 0)),
                pl.BlockSpec((PAIR, KEPT, size, size), lambda i, *_: (i, 0, 0, 0)),
            ],
            scratch_shapes=[
                pltpu.VMEM((slots + 1, size, width), jnp.bfloat16),
                pltpu.SemaphoreType.DMA((len(pieces),)),
            ],
        ),
        out_shape=[
            jax.ShapeDtypeStruct((width, width), jnp.float32),
            jax.ShapeDtypeStruct((count, KEPT, size, size), blocks.dtype),
        ],
        compiler_params=pltpu.CompilerParams(vmem_limit_bytes=EARLY_VMEM),
        cost_estimate=LIGHT,
        name="early_terms",
    )(spots, late, blocks, half, low, *as_blocks(pieces, size))


def late_terms(spots, late, fill, kept, blocks, half, low, pieces, places, slots):
    count, _, size, _ = blocks.shape
    width = half.shape[1]
    return pl.pallas_call(
        functools.partial(late_kernel, places),
        grid_spec=pltpu.PrefetchScalarGridSpec(
            num_scalar_prefetch=3,
            grid=(count // PAIR,),
            in_specs=[
                pl.BlockSpec((PAIR, KEPT, size, size), lambda i, *_: (i, 0, 0, 0)),
                pl.BlockSpec((PAIR * size, width), lambda i, *_: (i, 0)),
                pl.BlockSpec((PAIR * size, width), lambda i, *_: (i, 0)),
            ]
            + [pl.BlockSpec(memory_space=pl.ANY)] * (1 + len(pieces)),
            out_specs=pl.BlockSpec((width, width), lambda i, *_: (0, 0)),
            scratch_shapes=[
                pltpu.VMEM((slots + 1, size, width), jnp.bfloat16),
                pltpu.VMEM((size, size), blocks.dtype),
                pltpu.SemaphoreType.DMA((len(pieces),)),
                pltpu.SemaphoreType.DMA,
            ],
        ),
        out_shape=jax.ShapeDtypeStruct((width, width), jnp.float32),
        compiler_params=pltpu.CompilerParams(vmem_limit_bytes=LATE_VMEM),
        cost_estimate=LIGHT,
        name="late_terms",
    )(spots, late, fill, kept, half, low, blocks, *as_blocks(pieces, size))


def spread(value, axes):
    devices = lax.axis_size(axes)
    rows, width = value.shape
    copies = jnp.broadcast_to(value[None], (devices, rows, width))
    return lax.all_to_all(copies, axes, 0, 0, tiled=True).reshape(devices * rows, width)


def reduce_share(value, axes):
    devices = lax.axis_size(axes)
    rows, width = value.shape
    parts = lax.all_to_all(value.reshape(devices, rows // devices, width), axes, 0, 0, tiled=True)
    return parts.sum(axis=0)


def total(value):
    return spread(reduce_share(value, AXES), AXES)


def exchange(value, axes, mask):
    return lax.ppermute(value, axes, [(i, i ^ mask) for i in range(lax.axis_size(axes))])


def local(snapshots, blocks, columns):
    rows = snapshots.shape[0]
    size = blocks.shape[2]
    count = rows // size
    first, raw = FIRST * size, RAW * size
    partner_first = exchange(snapshots[:first], "yl", 1)
    share = reduce_share(local_gram(snapshots), SIDE)
    share, partner_first = lax.optimization_barrier((share, partner_first))
    near = [exchange(share, ("yh", "yl"), mask) for mask in (1, 2, 3)]
    share = (share + near[0]) + (near[1] + near[2])
    share, following = lax.optimization_barrier((share, snapshots[first:raw]))
    partner_second = exchange(following, "yl", 1)
    gram = spread(share, SIDE)
    total_rows = rows * lax.axis_size(AXES)
    scaled_factor, inverse = factorize(gram, 1.0 / math.sqrt(total_rows))
    late_half, half, low = late_basis(snapshots, inverse, raw)
    partner_late = exchange(late_half, "yl", 1)
    half, low, early_half = early_basis(snapshots, partner_first, partner_second, inverse, half, low)
    own = columns // count == lax.axis_index("yl")
    spots = columns % count + jnp.where(own, 0, count)
    slots = 2 * count
    is_late = spots >= count + RAW
    order = jnp.arange(columns.shape[1])
    ahead = is_late[:, None, :] & (order[None, None, :] < order[None, :, None])
    rank = jnp.where(is_late, ahead.sum(axis=2), slots)
    chosen = rank[:, None, :] == order[None, :, None]
    late = jnp.where(chosen, order[None, None, :], 0).sum(axis=2)
    fill = is_late.sum(axis=1)
    filled = order[None, :] < fill[:, None]
    late_spots = jnp.where(filled, jnp.where(chosen, spots[:, None, :], 0).sum(axis=2), slots)
    early, kept = early_terms(
        jnp.where(is_late, slots, spots), late, blocks, half, low,
        [half, early_half], [0, count], slots,
    )
    rest = late_terms(
        late_spots, late, fill, kept, blocks, half, low, [partner_late], [count + RAW], slots
    )
    projected = total(early + rest)
    return (projected, scaled_factor)


def solution(mesh):
    sizes = (4, 2, 4, 2, 2)
    fine = jax.sharding.Mesh(mesh.devices.reshape(sizes), AXES)
    return jax.shard_map(
        local,
        mesh=fine,
        in_specs=(
            P(AXES, None),
            P(AXES, None, None, None),
            P(AXES, None),
        ),
        out_specs=(P(), P()),
        check_vma=False,
    )
```

time: 1070 us -> 155 us (0.14); the launches traced: 1050 us -> 152 us
  other arithmetic: 289 us -> 0.63 us
  matrix products: 279 us -> 0 us
  waiting for transfers between devices: 229 us -> 11.8 us
  local copies, waits for them, and re-layouts: 203 us -> 9.13 us
  Pallas kernels: 0 us -> 62.3 us
  blocking collectives: 0 us -> 52.3 us
  between operations: 25.8 us -> 0.74 us
    another operation x55 -> x0, other arithmetic: 280 us -> none  [the longest x49 246 us: local(): factor = jnp.linalg.cholesky(combined).T]
    dot_general x274 -> x0, matrix products: 271 us -> none  [the longest x256 213 us: substitute(): jnp.dot(frow, inverse, precision=lax.Precision.HIGHEST)]
    dynamic_slice x256 -> x0, local copies, waits for them, and re-layouts: 152 us -> none  [substitute(): pivot = lax.dynamic_slice(factor, (index, index), (1, 1))]
    psum x1 -> x0, waiting for transfers between devices: 142 us -> none  [local(): projected = lax.psum(partial_terms, ('rows', 'grp'))]
    all_gather x1 -> x0, waiting for transfers between devices: 64.5 us -> none  [local(): gathered = lax.all_gather(basis_half, 'grp', axis=0, tiled=True)]
    pallas_call x0 -> x6, Pallas kernels: none -> 62.3 us  [the longest x1 18.5 us: early_terms(): pl.pallas_call(functools.partial(early_kernel, places), grid_spec=pltpu.P...]
    all_to_all x0 -> x3, blocking collectives: none -> 52.3 us  [the longest x2 37 us: reduce_share(): lax.all_to_all(value.reshape(devices, rows // devices, width), axes, 0, 0...]
    ppermute x7 -> x6, waiting for transfers between devices: 22.3 us -> 2.93 us  [exchange(): lax.ppermute(value, axes, [(i, i ^ mask) for i in range(lax.axis_size(axe...]
  transfers between devices with their start and end apart: 9 -> 7, of which waited for: 8 -> 3; matrix products, arithmetic and copies ran while one was open for 1% -> 1% of each run, Pallas kernels for 0% -> 33%
where the time goes in v1:
time: 155 us; the launch traced here: 152 us
  Pallas kernels  62.3 us (40%)
  blocking collectives  52.3 us (34%)
  starting transfers between devices  15.4 us (10%)
  waiting for transfers between devices  11.8 us (8%)
  local copies, waits for them, and re-layouts  9.13 us (6%)
    all_to_all x2, blocking collectives, reduce_share(): lax.all_to_all(value.reshape(devices, rows // devices, width), axes, 0, 0...  37 us
    pallas_call x1, Pallas kernels, early_terms(): pl.pallas_call(functools.partial(early_kernel, places), grid_spec=pltpu.P...  18.5 us
    all_to_all x1, blocking collectives, spread(): lax.all_to_all(copies, axes, 0, 0, tiled=True)  15.2 us
    pallas_call x1, Pallas kernels, late_terms(): pl.pallas_call(functools.partial(late_kernel, places), grid_spec=pltpu.Pr...  11.4 us
    pallas_call x1, Pallas kernels, factorize(): pl.pallas_call(functools.partial(factor_kernel, scale), out_shape=[jax.Sh...  10.1 us
    pallas_call x1, Pallas kernels, early_basis(): pl.pallas_call(functools.partial(early_basis_kernel, (own, mid)), grid=(2...  9.3 us
    all_to_all x1, starting transfers between devices, spread(): lax.all_to_all(copies, axes, 0, 0, tiled=True)  9.17 us
    all_to_all x1, waiting for transfers between devices, spread(): lax.all_to_all(copies, axes, 0, 0, tiled=True)  8.89 us
  transfers between devices with their start and end apart: 7, of which 3 were waited for; matrix products, arithmetic and copies ran while one was open for 1% of the time, Pallas kernels for 33%

profile of v1, /device:TPU:1, one launch (start us, length us, event | category | flops | bytes accessed | tf_op | source)
XLA Modules:
  0.0 152.4 jit_solution(4627439572638930371)
XLA Ops:
  0.6 1.7 %fusion.6 = (f32[1024,256]{1,0:T(8,128)S(1)}, f32[1024,256]{1,0:T(8,128)S(1)}) fusion(f32[4096,256]{1,0:T(8,128)} %x_ref.5), kind=kLoop, calls=%fused_computation.22 | loop fusion | bytes 4194304 | tf_op jit(solution)/shard_map/slice | solution.py:409
  2.3 2.2 %collective-permute-start = (f32[1024,256]{1,0:T(8,128)S(1)}, f32[1024,256]{1,0:T(8,128)}, u32[]{:S(2)}, u32[]{:S(2)}) collective-permute-start(f32[1024,256]{1,0:T(8,128)S(1)} %get-tuple-element.36), channel_id=1, source_target_pairs={{0,1},{1,0},{2,3},{3,2},{4,5},{5,4},{6,7},{7,6},{8,9},{9,8},{10,11... | collective-permute-start | bytes 3145736 | tf_op jit(solution)/shard_map/ppermute | solution.py:396
  4.5 7.6 %local_gram.1 = f32[256,256]{1,0:T(8,128)} custom-call(f32[4096,256]{1,0:T(8,128)} %x_ref.5), custom_call_target="tpu_custom_call" | custom-call | tf_op jit(solution)/shard_map/local_gram/pallas_call | solution.py:58
  12.1 18.0 %all_to_all.20 = f32[32,8,256]{2,1,0:T(8,128)S(1)} all-to-all(f32[32,8,256]{2,1,0:T(8,128)} %bitcast.8), channel_id=1, replica_groups=mesh['x'=4,'yh'=2,'z'=4,'core'=2,'yl'=2] {'x','z','core'}, dimensions={0} | all-to-all | bytes 524288 | tf_op jit(solution)/shard_map/all_to_all | solution.py:387
  30.1 0.2 collective-permute-start.1
  30.4 2.9 %collective-permute-start.2 = (f32[8,256]{1,0:T(8,128)S(1)}, f32[8,256]{1,0:T(8,128)S(1)}, u32[]{:S(2)}, u32[]{:S(2)}) collective-permute-start(f32[8,256]{1,0:T(8,128)S(1)} %reduce_sum.56), channel_id=1, source_target_pairs={{0,16},{1,17},{16,0},{17,1},{2,18},{3,19},{18,2},{19,3},{4,20},{5,... | collective-permute-start | bytes 24584 | tf_op jit(solution)/shard_map/ppermute | solution.py:396
  33.3 0.8 collective-permute-start.3
  34.1 0.3 collective-permute-done.2
  34.4 2.6 %collective-permute-done.3 = f32[8,256]{1,0:T(8,128)S(1)} collective-permute-done((f32[8,256]{1,0:T(8,128)S(1)}, f32[8,256]{1,0:T(8,128)S(1)}, u32[]{:S(2)}, u32[]{:S(2)}) %collective-permute-start.3) | collective-permute-done | bytes 8224 | tf_op jit(solution)/shard_map/ppermute | solution.py:396
  37.0 0.7 broadcast_in_dim.40
  37.7 9.2 %all-to-all-start.1 = ((f32[32,8,256]{2,1,0:T(8,128)}), f32[32,8,256]{2,1,0:T(8,128)S(1)}, u32[]{:S(2)}, u32[]{:S(2)}) async-start(f32[32,8,256]{2,1,0:T(8,128)} %broadcast_in_dim.40), calls=%async_computation.1 | async-start | bytes 524288 | tf_op jit(solution)/shard_map/all_to_all | solution.py:381
  47.0 8.9 %all-to-all-done.1 = f32[32,8,256]{2,1,0:T(8,128)S(1)} async-done(((f32[32,8,256]{2,1,0:T(8,128)}), f32[32,8,256]{2,1,0:T(8,128)S(1)}, u32[]{:S(2)}, u32[]{:S(2)}) %all-to-all-start.1) | async-done | bytes 262176 | tf_op jit(solution)/shard_map/all_to_all | solution.py:381
  55.9 0.7 copy-done.3
  56.6 10.1 %factorize.1 = (f32[256,256]{1,0:T(8,128)}, bf16[1536,256]{1,0:T(8,128)(2,1)}) custom-call(f32[256,256]{1,0:T(8,128)} %bitcast.9), custom_call_target="tpu_custom_call" | custom-call | tf_op jit(solution)/shard_map/factorize/pallas_call | solution.py:143
  66.7 5.4 %late_basis.1 = (bf16[2048,256]{1,0:T(8,128)(2,1)}, bf16[4096,256]{1,0:T(8,128)(2,1)}, bf16[4096,256]{1,0:T(8,128)(2,1)}) custom-call(f32[4096,256]{1,0:T(8,128)} %x_ref.5, bf16[1536,256]{1,0:T(8,128)(2,1)} %get-tuple-element.20.inv_ref), custom_call_target="tpu_custom_call" | custom-call | tf_op jit(solution)/shard_map/late_basis/pallas_call | solution.py:177
  73.1 9.3 %early_basis.1 = (bf16[4096,256]{1,0:T(8,128)(2,1)}, bf16[4096,256]{1,0:T(8,128)(2,1)}, bf16[2048,256]{1,0:T(8,128)(2,1)}) custom-call(f32[4096,256]{1,0:T(8,128)} %x_ref.5, f32[1024,256]{1,0:T(8,128)} %collective-permute-done.one_ref, f32[1024,256]{1,0:T(8,128)} %collective-permute-done.4.two_ref, ...), custom_call_target="tpu_custom_call", output_to_operand_aliasing={{0}: (4, {}), {1}: (5, {})} | custom-call | tf_op jit(solution)/shard_map/early_basis/pallas_call | solution.py:209
  82.4 1.6 %copy-done = bf16[4096,256]{1,0:T(8,128)(2,1)S(1)} copy-done((bf16[4096,256]{1,0:T(8,128)(2,1)S(1)}, bf16[4096,256]{1,0:T(8,128)(2,1)}, u32[]{:S(2)}) %copy-start) | copy-done | bytes 2097176
  84.0 1.6 %copy-done.1 = bf16[4096,256]{1,0:T(8,128)(2,1)S(1)} copy-done((bf16[4096,256]{1,0:T(8,128)(2,1)S(1)}, bf16[4096,256]{1,0:T(8,128)(2,1)}, u32[]{:S(2)}) %copy-start.1) | copy-done | bytes 2097176
  85.6 1.2 copy-done.2
  86.8 18.5 %early_terms.1 = (f32[256,256]{1,0:T(8,128)S(1)}, bf16[32,8,128,128]{3,2,1,0:T(8,128)(2,1)S(1)}) custom-call(s32[32,16]{1,0:T(8,128)S(1)} %get-tuple-element.38.spot_ref, s32[32,16]{1,0:T(8,128)S(1)} %copy.18.late_ref, bf16[32,16,128,128]{3,2,1,0:T(8,128)(2,1)} %blocks_ref.3, bf16[4096,256]{1,0:T(8,128)(2,1)S(1)} %copy-done, ...), custom_call_target="tpu_custom_call" | custom-call | tf_op jit(solution)/shard_map/early_terms/pallas_call | solution.py:318
  105.3 11.4 %late_terms.1 = f32[256,256]{1,0:T(8,128)S(1)} custom-call(s32[32,16]{1,0:T(8,128)S(1)} %fusion.3.spot_ref, s32[32,16]{1,0:T(8,128)S(1)} %copy.18.late_ref, s32[32]{0:T(128)S(1)} %get-tuple-element.32.fill_ref, bf16[32,8,128,128]{3,2,1,0:T(8,128)(2,1)S(1)} %get-tuple-element.27.kept_ref, bf16[4096,256]{1,0:T(8,128)(2,1)S(1)} %copy-done, ...), custom_call_target="tpu_custom_call" | custom-call | tf_op jit(solution)/shard_map/late_terms/pallas_call | solution.py:351
  117.0 19.0 %all_to_all.21 = f32[128,2,256]{2,1,0:T(2,128)S(1)} all-to-all(f32[128,2,256]{2,1,0:T(2,128)S(1)} %reshape.51), channel_id=1, replica_groups=mesh['x'=4,'yh'=2,'z'=4,'core'=2,'yl'=2] {'x','yh','z','core','yl'}, dimensions={0} | all-to-all | bytes 524288 | tf_op jit(solution)/shard_map/all_to_all | solution.py:387
  136.2 15.2 %all_to_all.22 = f32[128,2,256]{2,1,0:T(2,128)S(1)} all-to-all(f32[128,2,256]{2,1,0:T(2,128)S(1)} %broadcast_in_dim.59), channel_id=1, replica_groups=mesh['x'=4,'yh'=2,'z'=4,'core'=2,'yl'=2] {'x','yh','z','core','yl'}, dimensions={0} | all-to-all | bytes 524288 | tf_op jit(solution)/shard_map/all_to_all | solution.py:381
  151.5 0.9 reshape.52
  (31 shorter events, 1.5 us)
Async XLA Ops:
  2.3 27.8 %collective-permute-start = (f32[1024,256]{1,0:T(8,128)S(1)}, f32[1024,256]{1,0:T(8,128)}, u32[]{:S(2)}, u32[]{:S(2)}) collective-permute-start(f32[1024,256]{1,0:T(8,128)S(1)} %get-tuple-element.36), channel_id=1, source_target_pairs={{0,1},{1,0},{2,3},{3,2},{4,5},{5,4},{6,7},{7,6},{8,9},{9,8},{10,11... | collective-permute-start | bytes 3145736 | tf_op jit(solution)/shard_map/ppermute | solution.py:396
  12.1 60.0 %copy-start.4 = (s32[32,16]{0,1:T(8,128)S(1)}, s32[32,16]{0,1:T(8,128)}, u32[]{:S(2)}) copy-start(s32[32,16]{0,1:T(8,128)} %param.5) | copy-start | bytes 6148
  30.1 3.9 %collective-permute-start.1 = (f32[8,256]{1,0:T(8,128)S(1)}, f32[8,256]{1,0:T(8,128)S(1)}, u32[]{:S(2)}, u32[]{:S(2)}) collective-permute-start(f32[8,256]{1,0:T(8,128)S(1)} %reduce_sum.56), channel_id=1, source_target_pairs={{0,1},{1,0},{16,17},{17,16},{2,3},{3,2},{18,19},{19,18},{4,5},{5,4... | collective-permute-start | bytes 24584 | tf_op jit(solution)/shard_map/ppermute | solution.py:396
  30.4 4.0 %collective-permute-start.2 = (f32[8,256]{1,0:T(8,128)S(1)}, f32[8,256]{1,0:T(8,128)S(1)}, u32[]{:S(2)}, u32[]{:S(2)}) collective-permute-start(f32[8,256]{1,0:T(8,128)S(1)} %reduce_sum.56), channel_id=1, source_target_pairs={{0,16},{1,17},{16,0},{17,1},{2,18},{3,19},{18,2},{19,3},{4,20},{5,... | collective-permute-start | bytes 24584 | tf_op jit(solution)/shard_map/ppermute | solution.py:396
  33.3 3.7 %collective-permute-start.3 = (f32[8,256]{1,0:T(8,128)S(1)}, f32[8,256]{1,0:T(8,128)S(1)}, u32[]{:S(2)}, u32[]{:S(2)}) collective-permute-start(f32[8,256]{1,0:T(8,128)S(1)} %reduce_sum.56), channel_id=1, source_target_pairs={{0,17},{1,16},{16,1},{17,0},{2,19},{3,18},{18,3},{19,2},{4,21},{5,... | collective-permute-start | bytes 24584 | tf_op jit(solution)/shard_map/ppermute | solution.py:396
  37.7 18.2 %all-to-all-start.1 = ((f32[32,8,256]{2,1,0:T(8,128)}), f32[32,8,256]{2,1,0:T(8,128)S(1)}, u32[]{:S(2)}, u32[]{:S(2)}) async-start(f32[32,8,256]{2,1,0:T(8,128)} %broadcast_in_dim.40), calls=%async_computation.1 | async-start | bytes 524288 | tf_op jit(solution)/shard_map/all_to_all | solution.py:381
  46.9 26.2 %collective-permute-start.4 = (f32[1024,256]{1,0:T(8,128)S(1)}, f32[1024,256]{1,0:T(8,128)}, u32[]{:S(2)}, u32[]{:S(2)}) collective-permute-start(f32[1024,256]{1,0:T(8,128)S(1)} %get-tuple-element.18), channel_id=1, source_target_pairs={{0,1},{1,0},{2,3},{3,2},{4,5},{5,4},{6,7},{7,6},{8,9},{9,8},{10,11... | collective-permute-start | bytes 3145736 | tf_op jit(solution)/shard_map/ppermute | solution.py:396
  55.9 0.7 copy-start.3
  72.1 33.2 %collective-permute-start.5 = (bf16[2048,256]{1,0:T(8,128)(2,1)}, bf16[2048,256]{1,0:T(8,128)(2,1)S(1)}, u32[]{:S(2)}, u32[]{:S(2)}) collective-permute-start(bf16[2048,256]{1,0:T(8,128)(2,1)} %get-tuple-element.28), channel_id=1, source_target_pairs={{0,1},{1,0},{2,3},{3,2},{4,5},{5,4},{6,7},{7,6},{8,9},{9,8},{10,11... | collective-permute-start | bytes 3145736 | tf_op jit(solution)/shard_map/ppermute | solution.py:396
  82.4 1.6 %copy-start = (bf16[4096,256]{1,0:T(8,128)(2,1)S(1)}, bf16[4096,256]{1,0:T(8,128)(2,1)}, u32[]{:S(2)}) copy-start(bf16[4096,256]{1,0:T(8,128)(2,1)} %get-tuple-element.23.half_ref) | copy-start | bytes 6291460
  84.0 1.6 %copy-start.1 = (bf16[4096,256]{1,0:T(8,128)(2,1)S(1)}, bf16[4096,256]{1,0:T(8,128)(2,1)}, u32[]{:S(2)}) copy-start(bf16[4096,256]{1,0:T(8,128)(2,1)} %get-tuple-element.24.low_ref) | copy-start | bytes 6291460
  85.5 1.2 copy-start.2

commit v2 on v1

v2 whole, which is shorter than its diff:
```python
import functools
import math

import jax
import jax.numpy as jnp
from jax import lax
from jax.experimental import pallas as pl
from jax.experimental.pallas import tpu as pltpu
from jax.sharding import PartitionSpec as P

HIGHEST = lax.Precision.HIGHEST
AXES = ("x", "yh", "z", "core", "yl")
SIDE = ("x", "z", "core")
PANEL = 64
FIRST = 8
RAW = 16
GRAM_TILE = 2048
ROW_TILE = 1024
PAIR = 8
LIGHT = pl.CostEstimate(flops=0, transcendentals=0, bytes_accessed=0)
EARLY_VMEM = 56 << 20


def tdot(left, right):
    return lax.dot_general(left, right, (((0,), (0,)), ((), ())), preferred_element_type=jnp.float32)


def thirds(value):
    high = value.astype(jnp.bfloat16)
    rest = value - high.astype(jnp.float32)
    mid = rest.astype(jnp.bfloat16)
    low = (rest - mid.astype(jnp.float32)).astype(jnp.bfloat16)
    return high, mid, low


def gram_kernel(x_ref, g_ref, sym_ref, off_ref):
    step = pl.program_id(0)

    @pl.when(step == 0)
    def _():
        sym_ref[...] = jnp.zeros_like(sym_ref)
        off_ref[...] = jnp.zeros_like(off_ref)

    high, mid, low = thirds(x_ref[...])
    both = jnp.concatenate([high, mid], axis=0)
    sym_ref[...] += tdot(both, both)
    off_ref[...] += tdot(jnp.concatenate([high, high], axis=0), jnp.concatenate([mid, low], axis=0))

    @pl.when(step == pl.num_programs(0) - 1)
    def _():
        off = off_ref[...]
        g_ref[...] = sym_ref[...] + (off + off.T)


def local_gram(snapshots):
    rows, width = snapshots.shape
    return pl.pallas_call(
        gram_kernel,
        grid=(rows // GRAM_TILE,),
        in_specs=[pl.BlockSpec((GRAM_TILE, width), lambda i: (i, 0))],
        out_specs=pl.BlockSpec((width, width), lambda i: (0, 0)),
        out_shape=jax.ShapeDtypeStruct((width, width), jnp.float32),
        scratch_shapes=[pltpu.VMEM((width, width), jnp.float32)] * 2,
        cost_estimate=LIGHT,
        name="local_gram",
    )(snapshots)


def factor_kernel(scale, g_ref, sf_ref, inv_ref, r_ref, l_ref):
    n = g_ref.shape[0]
    sub = lax.broadcasted_iota(jnp.int32, (8, 128), 0)
    lane = lax.broadcasted_iota(jnp.int32, (8, 128), 1)
    r_ref[...] = jnp.zeros_like(r_ref)
    l_ref[...] = jnp.zeros_like(l_ref)
    for r0 in range(0, n, PANEL):
        first = r0 // 128
        keys = [("r", i) for i in range(first, n // 128)] + [("l", i) for i in range(first + 1)]
        depth = -(-r0 // 128) * 128
        left = None
        if depth:
            a = first * 128
            left = r_ref[0:depth, a:a + 128].T[r0 - a:r0 - a + PANEL, :]
        tile = {}
        for key in keys:
            kind, i = key
            if kind == "r":
                part = g_ref[r0:r0 + PANEL, i * 128:(i + 1) * 128]
            else:
                rows = lax.broadcasted_iota(jnp.int32, (PANEL, 128), 0) + r0
                cols = lax.broadcasted_iota(jnp.int32, (PANEL, 128), 1) + i * 128
                part = jnp.where(rows == cols, 1.0, 0.0).astype(jnp.float32)
            if depth:
                right = (r_ref if kind == "r" else l_ref)[0:depth, i * 128:(i + 1) * 128]
                part = part - jnp.dot(left, right, precision=HIGHEST, preferred_element_type=jnp.float32)
            for t in range(PANEL // 8):
                tile[t, key] = part[t * 8:(t + 1) * 8, :]
        pk = ("r", first)
        nt = PANEL // 8
        for tk in range(nt):
            c0 = (r0 + tk * 8) % 128
            cols = {}
            for q in range(8):
                for t in range(tk, nt):
                    cols[t, q] = jnp.broadcast_to(tile[t, pk][:, c0 + q:c0 + q + 1], (8, 128))
            rows = {}
            for q in range(8):
                pivot = jnp.broadcast_to(cols[tk, q][q:q + 1, :], (8, 128))
                recip = 1.0 / pivot
                for key in keys:
                    rows[q, key] = jnp.broadcast_to(tile[tk, key][q:q + 1, :], (8, 128)) * recip
                below = jnp.where(sub > q, cols[tk, q], 0.0)
                if q < 7:
                    for key in keys:
                        tile[tk, key] = tile[tk, key] - below * rows[q, key]
                for p in range(q + 1, 8):
                    coef = jnp.broadcast_to(cols[tk, p][q:q + 1, :], (8, 128)) * recip
                    cols[tk, p] = cols[tk, p] - below * coef
                    for t in range(tk + 1, nt):
                        cols[t, p] = cols[t, p] - cols[t, q] * coef
            for t in range(tk + 1, nt):
                for key in keys:
                    acc = tile[t, key]
                    for q in range(8):
                        acc = acc - cols[t, q] * rows[q, key]
                    tile[t, key] = acc
        for t in range(nt):
            at = sub + (r0 + t * 8 - first * 128)
            diag = jnp.sum(jnp.where(lane == at, tile[t, pk], 0.0), axis=1, keepdims=True)
            scale_rows = jnp.broadcast_to(1.0 / jnp.sqrt(diag), (8, 128))
            for key in keys:
                value = tile[t, key] * scale_rows
                if key == pk:
                    value = jnp.where(lane >= at, value, 0.0)
                (r_ref if key[0] == "r" else l_ref)[r0 + t * 8:r0 + t * 8 + 8, key[1] * 128:(key[1] + 1) * 128] = value
    sf_ref[...] = r_ref[...] * scale
    high, mid, low = thirds(l_ref[...].T)
    for at, part in enumerate([high, mid, low, high, mid, high]):
        inv_ref[at * n:(at + 1) * n, :] = part

def factorize(gram, scale):
    size = gram.shape[0]
    return pl.pallas_call(
        functools.partial(factor_kernel, scale),
        out_shape=[
            jax.ShapeDtypeStruct((size, size), jnp.float32),
            jax.ShapeDtypeStruct((6 * size, size), jnp.bfloat16),
        ],
        in_specs=[pl.BlockSpec(memory_space=pltpu.VMEM)],
        out_specs=[pl.BlockSpec(memory_space=pltpu.VMEM)] * 2,
        scratch_shapes=[pltpu.VMEM((size, size), jnp.float32)] * 2,
        cost_estimate=LIGHT,
        name="factorize",
    )(gram)


def basis_of(value, inverse):
    high, mid, low = thirds(value)
    terms = jnp.concatenate([low, mid, high, mid, high, high], axis=1)
    return jnp.dot(terms, inverse, preferred_element_type=jnp.float32)


def own_basis_kernel(x_ref, inv_ref, *refs):
    half_ref, turned_ref = refs[-2:]
    basis = basis_of(x_ref[...], inv_ref[...])
    half = basis.astype(jnp.bfloat16)
    half_ref[...] = half
    if len(refs) == 3:
        refs[0][...] = half
    turned = basis.T
    high = turned.astype(jnp.bfloat16)
    rest = (turned - high.astype(jnp.float32)).astype(jnp.bfloat16)
    size = turned_ref.shape[2] // 2
    for i in range(turned_ref.shape[0]):
        span = slice(i * size, (i + 1) * size)
        turned_ref[i] = jnp.concatenate([high[:, span], rest[:, span]], axis=1)


def own_basis(snapshots, inverse, start, stop, size, held=None):
    rows, width = snapshots.shape
    tile = math.gcd(math.gcd(start, stop), ROW_TILE)
    first = start // tile
    shifted = pl.BlockSpec((tile, width), lambda i: (i + first, 0))
    half = jax.ShapeDtypeStruct((rows, width), jnp.bfloat16)
    turned = jax.ShapeDtypeStruct((rows // size, width, 2 * size), jnp.bfloat16)
    out_specs = [shifted, pl.BlockSpec((tile // size, width, 2 * size), lambda i: (i + first, 0, 0))]
    out_shape = [half, turned]
    if held is None:
        out_specs = [pl.BlockSpec((tile, width), lambda i: (i, 0))] + out_specs
        out_shape = [jax.ShapeDtypeStruct((stop - start, width), jnp.bfloat16)] + out_shape
    held = held or []
    return pl.pallas_call(
        own_basis_kernel,
        grid=((stop - start) // tile,),
        in_specs=[shifted, pl.BlockSpec(inverse.shape, lambda i: (0, 0))]
        + [pl.BlockSpec(memory_space=pl.ANY)] * len(held),
        out_specs=out_specs,
        out_shape=out_shape,
        input_output_aliases={2 + i: i for i in range(len(held))},
        cost_estimate=LIGHT,
        name="own_basis",
    )(snapshots, inverse, *held)


def other_basis_kernel(switch, one_ref, two_ref, inv_ref, out_ref):
    value = jnp.where(pl.program_id(0) < switch, one_ref[...], two_ref[...])
    out_ref[...] = basis_of(value, inv_ref[...]).astype(jnp.bfloat16)


def other_basis(one, two, inverse):
    width = one.shape[1]
    tile = math.gcd(math.gcd(one.shape[0], two.shape[0]), ROW_TILE)
    switch, steps = one.shape[0] // tile, (one.shape[0] + two.shape[0]) // tile
    return pl.pallas_call(
        functools.partial(other_basis_kernel, switch),
        grid=(steps,),
        in_specs=[
            pl.BlockSpec((tile, width), lambda i: (jnp.minimum(i, switch - 1), 0)),
            pl.BlockSpec((tile, width), lambda i: (jnp.maximum(i - switch, 0), 0)),
            pl.BlockSpec(inverse.shape, lambda i: (0, 0)),
        ],
        out_specs=pl.BlockSpec((tile, width), lambda i: (i, 0)),
        out_shape=jax.ShapeDtypeStruct((steps * tile, width), jnp.bfloat16),
        cost_estimate=LIGHT,
        name="other_basis",
    )(one, two, inverse)


def split_pair(value):
    high = value.astype(jnp.bfloat16)
    rest = (value - high.astype(jnp.float32)).astype(jnp.bfloat16)
    return jnp.concatenate([high, rest], axis=1)


def doubled(half):
    return jnp.concatenate([half, half], axis=0)


def early_kernel(places, spot_ref, blocks_ref, turned_ref, *refs):
    pieces, (out_ref, left_ref, sums_ref, window_ref, sems) = refs[:-5], refs[-5:]
    step = pl.program_id(0)
    size = blocks_ref.shape[2]
    copies = [
        pltpu.make_async_copy(piece, window_ref.at[pl.ds(at, piece.shape[0])], sems.at[i])
        for i, (piece, at) in enumerate(zip(pieces, places))
    ]

    @pl.when(step == 0)
    def _():
        for copy in copies:
            copy.start()
        sums_ref[...] = jnp.zeros_like(sums_ref)

    for row in range(PAIR):
        at = step * PAIR + row
        for j in range(0, blocks_ref.shape[1], 2):
            pair = jnp.concatenate([blocks_ref[row, j], blocks_ref[row, j + 1]], axis=1)
            term = jnp.dot(turned_ref[row], doubled(pair), preferred_element_type=jnp.float32)
            sums_ref[spot_ref[at, j]] += term[:, :size]
            sums_ref[spot_ref[at, j + 1]] += term[:, size:]

    @pl.when(step == pl.num_programs(0) - 1)
    def _():
        for copy in copies:
            copy.wait()
        known = window_ref.shape[0]
        total = jnp.zeros_like(out_ref)
        for c in range(known):
            total += jnp.dot(
                split_pair(sums_ref[c]), doubled(window_ref[c]), preferred_element_type=jnp.float32
            )
        out_ref[...] = total
        for c in range(left_ref.shape[0]):
            left_ref[c] = split_pair(sums_ref[known + c])


def early_terms(spots, blocks, turned, pieces, slots):
    count, stored, size, _ = blocks.shape
    width = turned.shape[1]
    pieces = [piece.reshape(piece.shape[0] // size, size, width) for piece in pieces]
    places = [sum(piece.shape[0] for piece in pieces[:i]) for i in range(len(pieces))]
    known = places[-1] + pieces[-1].shape[0]
    return pl.pallas_call(
        functools.partial(early_kernel, places),
        grid_spec=pltpu.PrefetchScalarGridSpec(
            num_scalar_prefetch=1,
            grid=(count // PAIR,),
            in_specs=[
                pl.BlockSpec((PAIR, stored, size, size), lambda i, *_: (i, 0, 0, 0)),
                pl.BlockSpec((PAIR, width, 2 * size), lambda i, *_: (i, 0, 0)),
            ]
            + [pl.BlockSpec(memory_space=pl.ANY)] * len(pieces),
            out_specs=[
                pl.BlockSpec((width, width), lambda i, *_: (0, 0)),
                pl.BlockSpec((slots - known, width, 2 * size), lambda i, *_: (0, 0, 0)),
            ],
            scratch_shapes=[
                pltpu.VMEM((slots, width, size), jnp.float32),
                pltpu.VMEM((known, size, width), jnp.bfloat16),
                pltpu.SemaphoreType.DMA((len(pieces),)),
            ],
        ),
        out_shape=[
            jax.ShapeDtypeStruct((width, width), jnp.float32),
            jax.ShapeDtypeStruct((slots - known, width, 2 * size), jnp.bfloat16),
        ],
        compiler_params=pltpu.CompilerParams(vmem_limit_bytes=EARLY_VMEM),
        cost_estimate=LIGHT,
        name="early_terms",
    )(spots, blocks, turned, *pieces)


def late_kernel(early_ref, left_ref, half_ref, out_ref):
    total = early_ref[...]
    for c in range(left_ref.shape[0]):
        total += jnp.dot(left_ref[c], doubled(half_ref[c]), preferred_element_type=jnp.float32)
    out_ref[...] = total


def late_terms(early, left, half):
    size = left.shape[2] // 2
    return pl.pallas_call(
        late_kernel,
        in_specs=[pl.BlockSpec(memory_space=pltpu.VMEM)] * 3,
        out_specs=pl.BlockSpec(memory_space=pltpu.VMEM),
        out_shape=jax.ShapeDtypeStruct(early.shape, jnp.float32),
        cost_estimate=LIGHT,
        name="late_terms",
    )(early, left, half.reshape(left.shape[0], size, half.shape[1]))


def spread(value, axes):
    devices = lax.axis_size(axes)
    rows, width = value.shape
    copies = jnp.broadcast_to(value[None], (devices, rows, width))
    return lax.all_to_all(copies, axes, 0, 0, tiled=True).reshape(devices * rows, width)


def reduce_share(value, axes):
    devices = lax.axis_size(axes)
    rows, width = value.shape
    parts = lax.all_to_all(value.reshape(devices, rows // devices, width), axes, 0, 0, tiled=True)
    return parts.sum(axis=0)


def total(value):
    return spread(reduce_share(value, AXES), AXES)


def exchange(value, axes, mask):
    return lax.ppermute(value, axes, [(i, i ^ mask) for i in range(lax.axis_size(axes))])


def local(snapshots, blocks, columns):
    rows = snapshots.shape[0]
    size = blocks.shape[2]
    count = rows // size
    first, raw = FIRST * size, RAW * size
    partner_first = exchange(snapshots[:first], "yl", 1)
    share = reduce_share(local_gram(snapshots), SIDE)
    share, partner_first = lax.optimization_barrier((share, partner_first))
    near = [exchange(share, ("yh", "yl"), mask) for mask in (1, 2, 3)]
    share = (share + near[0]) + (near[1] + near[2])
    share, following = lax.optimization_barrier((share, snapshots[first:raw]))
    partner_second = exchange(following, "yl", 1)
    gram = spread(share, SIDE)
    total_rows = rows * lax.axis_size(AXES)
    scaled_factor, inverse = factorize(gram, 1.0 / math.sqrt(total_rows))
    late_half, half, turned = own_basis(snapshots, inverse, raw, rows, size)
    partner_late = exchange(late_half, "yl", 1)
    half, turned = own_basis(snapshots, inverse, 0, raw, size, [half, turned])
    other_half = other_basis(partner_first, partner_second, inverse)
    own = columns // count == lax.axis_index("yl")
    spots = columns % count + jnp.where(own, 0, count)
    early, left = early_terms(spots, blocks, turned, [half, other_half], 2 * count)
    projected = total(late_terms(early, left, partner_late))
    return (projected, scaled_factor)


def solution(mesh):
    sizes = (4, 2, 4, 2, 2)
    fine = jax.sharding.Mesh(mesh.devices.reshape(sizes), AXES)
    return jax.shard_map(
        local,
        mesh=fine,
        in_specs=(
            P(AXES, None),
            P(AXES, None, None, None),
            P(AXES, None),
        ),
        out_specs=(P(), P()),
        check_vma=False,
    )
```

time: 155 us -> 140 us (0.903); the launches traced: 152 us -> 139 us
  Pallas kernels: 62.3 us -> 52.4 us
  blocking collectives: 52.3 us -> 49.8 us
  local copies, waits for them, and re-layouts: 9.13 us -> 7.17 us
    pallas_call x4 -> x5, Pallas kernels: 33.7 us -> 22.7 us  [the longest x2 9.69 us: own_basis(): pl.pallas_call(own_basis_kernel, grid=((stop - start) // tile,), in_specs...]
    unnamed x11 -> x9, local copies, waits for them, and re-layouts: 5.19 us -> 1.75 us
    all_to_all x2, blocking collectives: 37 us -> 34.5 us  [reduce_share(): lax.all_to_all(value.reshape(devices, rows // devices, width), axes, 0, 0...]
    all_to_all x1, starting transfers between devices: 9.17 us -> 10.9 us  [spread(): lax.all_to_all(copies, axes, 0, 0, tiled=True)]
  transfers between devices with their start and end apart: 7 -> 7, of which waited for: 3 -> 3; matrix products, arithmetic and copies ran while one was open for 1% -> 1% of each run, Pallas kernels for 33% -> 35%
where the time goes in v2:
time: 140 us; the launch traced here: 139 us
  Pallas kernels  52.4 us (37%)
  blocking collectives  49.8 us (36%)
  starting transfers between devices  16.4 us (12%)
  waiting for transfers between devices  12.1 us (9%)
  local copies, waits for them, and re-layouts  7.17 us (5%)
    all_to_all x2, blocking collectives, reduce_share(): lax.all_to_all(value.reshape(devices, rows // devices, width), axes, 0, 0...  34.5 us
    pallas_call x1, Pallas kernels, early_terms(): pl.pallas_call(functools.partial(early_kernel, places), grid_spec=pltpu.P...  19.6 us
    all_to_all x1, blocking collectives, spread(): lax.all_to_all(copies, axes, 0, 0, tiled=True)  15.2 us
    all_to_all x1, starting transfers between devices, spread(): lax.all_to_all(copies, axes, 0, 0, tiled=True)  10.9 us
    pallas_call x1, Pallas kernels, factorize(): pl.pallas_call(functools.partial(factor_kernel, scale), out_shape=[jax.Sh...  10.1 us
    pallas_call x2, Pallas kernels, own_basis(): pl.pallas_call(own_basis_kernel, grid=((stop - start) // tile,), in_specs...  9.69 us
    all_to_all x1, waiting for transfers between devices, spread(): lax.all_to_all(copies, axes, 0, 0, tiled=True)  8.89 us
    ppermute x6, starting transfers between devices, exchange(): lax.ppermute(value, axes, [(i, i ^ mask) for i in range(lax.axis_size(axe...  5.55 us
  transfers between devices with their start and end apart: 7, of which 3 were waited for; matrix products, arithmetic and copies ran while one was open for 1% of the time, Pallas kernels for 35%

profile of v2, /device:TPU:1, one launch (start us, length us, event | category | flops | bytes accessed | tf_op | source)
XLA Modules:
  0.0 139.5 jit_solution(14480915564413055349)
XLA Ops:
  0.6 2.6 %fusion.4 = (f32[1024,256]{1,0:T(8,128)S(1)}, f32[1024,256]{1,0:T(8,128)}) fusion(f32[4096,256]{1,0:T(8,128)} %x_ref.5), kind=kLoop, calls=%fused_computation.11 | loop fusion | bytes 4194304 | tf_op jit(solution)/shard_map/slice | solution.py:363
  3.3 2.1 %collective-permute-start = (f32[1024,256]{1,0:T(8,128)}, f32[1024,256]{1,0:T(8,128)S(1)}, u32[]{:S(2)}, u32[]{:S(2)}) collective-permute-start(f32[1024,256]{1,0:T(8,128)} %get-tuple-element.29), channel_id=1, source_target_pairs={{0,1},{1,0},{2,3},{3,2},{4,5},{5,4},{6,7},{7,6},{8,9},{9,8},{10,11... | collective-permute-start | bytes 3145736 | tf_op jit(solution)/shard_map/ppermute | solution.py:350
  5.4 5.1 %local_gram.1 = f32[256,256]{1,0:T(8,128)} custom-call(f32[4096,256]{1,0:T(8,128)} %x_ref.5), custom_call_target="tpu_custom_call" | custom-call | tf_op jit(solution)/shard_map/local_gram/pallas_call | solution.py:57
  10.5 18.0 %all_to_all.20 = f32[32,8,256]{2,1,0:T(8,128)S(1)} all-to-all(f32[32,8,256]{2,1,0:T(8,128)} %bitcast.8), channel_id=1, replica_groups=mesh['x'=4,'yh'=2,'z'=4,'core'=2,'yl'=2] {'x','z','core'}, dimensions={0} | all-to-all | bytes 524288 | tf_op jit(solution)/shard_map/all_to_all | solution.py:341
  28.5 2.6 %collective-permute-start.3 = (f32[8,256]{1,0:T(8,128)S(1)}, f32[8,256]{1,0:T(8,128)S(1)}, u32[]{:S(2)}, u32[]{:S(2)}) collective-permute-start(f32[8,256]{1,0:T(8,128)S(1)} %reduce_sum.18), channel_id=1, source_target_pairs={{0,17},{1,16},{16,1},{17,0},{2,19},{3,18},{18,3},{19,2},{4,21},{5,... | collective-permute-start | bytes 24584 | tf_op jit(solution)/shard_map/ppermute | solution.py:350
  31.4 0.4 collective-permute-start.1
  31.9 0.5 collective-permute-done.3
  32.3 2.8 %collective-permute-done.2 = f32[8,256]{1,0:T(8,128)S(1)} collective-permute-done((f32[8,256]{1,0:T(8,128)S(1)}, f32[8,256]{1,0:T(8,128)S(1)}, u32[]{:S(2)}, u32[]{:S(2)}) %collective-permute-start.2) | collective-permute-done | bytes 8224 | tf_op jit(solution)/shard_map/ppermute | solution.py:350
  35.1 0.7 broadcast_in_dim.8
  35.8 10.9 %all-to-all-start.1 = ((f32[32,8,256]{2,1,0:T(8,128)}), f32[32,8,256]{2,1,0:T(8,128)S(1)}, u32[]{:S(2)}, u32[]{:S(2)}) async-start(f32[32,8,256]{2,1,0:T(8,128)} %broadcast_in_dim.8), calls=%async_computation.1 | async-start | bytes 524288 | tf_op jit(solution)/shard_map/all_to_all | solution.py:335
  46.8 8.9 %all-to-all-done.1 = f32[32,8,256]{2,1,0:T(8,128)S(1)} async-done(((f32[32,8,256]{2,1,0:T(8,128)}), f32[32,8,256]{2,1,0:T(8,128)S(1)}, u32[]{:S(2)}, u32[]{:S(2)}) %all-to-all-start.1) | async-done | bytes 262176 | tf_op jit(solution)/shard_map/all_to_all | solution.py:335
  55.7 0.7 copy-done.1
  56.4 10.1 %factorize.1 = (f32[256,256]{1,0:T(8,128)}, bf16[1536,256]{1,0:T(8,128)(2,1)}) custom-call(f32[256,256]{1,0:T(8,128)} %bitcast.9), custom_call_target="tpu_custom_call" | custom-call | tf_op jit(solution)/shard_map/factorize/pallas_call | solution.py:142
  66.5 5.0 %own_basis.2 = (bf16[2048,256]{1,0:T(8,128)(2,1)}, bf16[4096,256]{1,0:T(8,128)(2,1)}, bf16[32,256,256]{2,1,0:T(8,128)(2,1)}) custom-call(f32[4096,256]{1,0:T(8,128)} %x_ref.5, bf16[1536,256]{1,0:T(8,128)(2,1)} %get-tuple-element.17.inv_ref), custom_call_target="tpu_custom_call" | custom-call | tf_op jit(solution)/shard_map/own_basis/pallas_call | solution.py:191
  71.6 0.6 fusion.spot_ref
  72.2 4.7 %own_basis.3 = (bf16[4096,256]{1,0:T(8,128)(2,1)}, bf16[32,256,256]{2,1,0:T(8,128)(2,1)}) custom-call(f32[4096,256]{1,0:T(8,128)} %x_ref.5, bf16[1536,256]{1,0:T(8,128)(2,1)} %get-tuple-element.17.inv_ref, bf16[4096,256]{1,0:T(8,128)(2,1)} %get-tuple-element.18.refs_0_, ...), custom_call_target="tpu_custom_call", output_to_operand_aliasing={{0}: (2, {}), {1}: (3, {})} | custom-call | tf_op jit(solution)/shard_map/own_basis/pallas_call | solution.py:191
  77.0 4.6 %other_basis.1 = bf16[2048,256]{1,0:T(8,128)(2,1)} custom-call(f32[1024,256]{1,0:T(8,128)} %copy-done.2, f32[1024,256]{1,0:T(8,128)} %collective-permute-done.4.two_ref, bf16[1536,256]{1,0:T(8,128)(2,1)} %get-tuple-element.17.inv_ref), custom_call_target="tpu_custom_call" | custom-call | tf_op jit(solution)/shard_map/other_basis/pallas_call | solution.py:213
  81.6 19.6 %early_terms.1 = (f32[256,256]{1,0:T(8,128)}, bf16[16,256,256]{2,1,0:T(8,128)(2,1)}) custom-call(s32[32,16]{1,0:T(8,128)} %fusion.spot_ref, bf16[32,16,128,128]{3,2,1,0:T(8,128)(2,1)} %blocks_ref.1, bf16[32,256,256]{2,1,0:T(8,128)(2,1)} %get-tuple-element.20.turned_ref, bf16[32,128,256]{2,1,0:T(8,128)(2,1)} %bitcast.5, bf16[16,128,256]{2,1,0:T(8,128)(2,1)} %bitcast.6), custom_call_target="tpu_custom_call" | custom-call | tf_op jit(solution)/shard_map/early_terms/pallas_call | solution.py:282
  101.2 1.0 copy-done
  102.1 3.3 %late_terms.1 = f32[256,256]{1,0:T(8,128)} custom-call(f32[256,256]{1,0:T(8,128)} %get-tuple-element.24.early_ref, bf16[16,256,256]{2,1,0:T(8,128)(2,1)} %get-tuple-element.25.left_ref, bf16[16,128,256]{2,1,0:T(8,128)(2,1)} %bitcast.7), custom_call_target="tpu_custom_call" | custom-call | tf_op jit(solution)/shard_map/late_terms/pallas_call | solution.py:321
  105.5 1.1 reshape.32
  106.6 16.5 %all_to_all.21 = f32[128,2,256]{2,1,0:T(2,128)S(1)} all-to-all(f32[128,2,256]{2,1,0:T(2,128)S(1)} %reshape.32), channel_id=1, replica_groups=mesh['x'=4,'yh'=2,'z'=4,'core'=2,'yl'=2] {'x','yh','z','core','yl'}, dimensions={0} | all-to-all | bytes 524288 | tf_op jit(solution)/shard_map/all_to_all | solution.py:341
  123.3 15.2 %all_to_all.22 = f32[128,2,256]{2,1,0:T(2,128)S(1)} all-to-all(f32[128,2,256]{2,1,0:T(2,128)S(1)} %broadcast_in_dim.9), channel_id=1, replica_groups=mesh['x'=4,'yh'=2,'z'=4,'core'=2,'yl'=2] {'x','yh','z','core','yl'}, dimensions={0} | all-to-all | bytes 524288 | tf_op jit(solution)/shard_map/all_to_all | solution.py:335
  138.6 0.9 reshape.33
  (18 shorter events, 0.8 us)
Async XLA Ops:
  3.3 25.2 %collective-permute-start = (f32[1024,256]{1,0:T(8,128)}, f32[1024,256]{1,0:T(8,128)S(1)}, u32[]{:S(2)}, u32[]{:S(2)}) collective-permute-start(f32[1024,256]{1,0:T(8,128)} %get-tuple-element.29), channel_id=1, source_target_pairs={{0,1},{1,0},{2,3},{3,2},{4,5},{5,4},{6,7},{7,6},{8,9},{9,8},{10,11... | collective-permute-start | bytes 3145736 | tf_op jit(solution)/shard_map/ppermute | solution.py:350
  10.5 61.1 %copy-start.3 = (s32[32,16]{0,1:T(8,128)S(1)}, s32[32,16]{0,1:T(8,128)}, u32[]{:S(2)}) copy-start(s32[32,16]{0,1:T(8,128)} %param.5) | copy-start | bytes 6148
  28.5 48.4 %copy-start.2 = (f32[1024,256]{1,0:T(8,128)}, f32[1024,256]{1,0:T(8,128)S(1)}, u32[]{:S(2)}) copy-start(f32[1024,256]{1,0:T(8,128)S(1)} %collective-permute-done.one_ref) | copy-start | bytes 3145732
  28.5 3.8 %collective-permute-start.3 = (f32[8,256]{1,0:T(8,128)S(1)}, f32[8,256]{1,0:T(8,128)S(1)}, u32[]{:S(2)}, u32[]{:S(2)}) collective-permute-start(f32[8,256]{1,0:T(8,128)S(1)} %reduce_sum.18), channel_id=1, source_target_pairs={{0,17},{1,16},{16,1},{17,0},{2,19},{3,18},{18,3},{19,2},{4,21},{5,... | collective-permute-start | bytes 24584 | tf_op jit(solution)/shard_map/ppermute | solution.py:350
  31.1 4.0 %collective-permute-start.2 = (f32[8,256]{1,0:T(8,128)S(1)}, f32[8,256]{1,0:T(8,128)S(1)}, u32[]{:S(2)}, u32[]{:S(2)}) collective-permute-start(f32[8,256]{1,0:T(8,128)S(1)} %reduce_sum.18), channel_id=1, source_target_pairs={{0,16},{1,17},{16,0},{17,1},{2,18},{3,19},{18,2},{19,3},{4,20},{5,... | collective-permute-start | bytes 24584 | tf_op jit(solution)/shard_map/ppermute | solution.py:350
  31.4 3.7 %collective-permute-start.1 = (f32[8,256]{1,0:T(8,128)S(1)}, f32[8,256]{1,0:T(8,128)S(1)}, u32[]{:S(2)}, u32[]{:S(2)}) collective-permute-start(f32[8,256]{1,0:T(8,128)S(1)} %reduce_sum.18), channel_id=1, source_target_pairs={{0,1},{1,0},{16,17},{17,16},{2,3},{3,2},{18,19},{19,18},{4,5},{5,4... | collective-permute-start | bytes 24584 | tf_op jit(solution)/shard_map/ppermute | solution.py:350
  35.8 19.9 %all-to-all-start.1 = ((f32[32,8,256]{2,1,0:T(8,128)}), f32[32,8,256]{2,1,0:T(8,128)S(1)}, u32[]{:S(2)}, u32[]{:S(2)}) async-start(f32[32,8,256]{2,1,0:T(8,128)} %broadcast_in_dim.8), calls=%async_computation.1 | async-start | bytes 524288 | tf_op jit(solution)/shard_map/all_to_all | solution.py:335
  46.7 30.2 %collective-permute-start.4 = (f32[1024,256]{1,0:T(8,128)S(1)}, f32[1024,256]{1,0:T(8,128)}, u32[]{:S(2)}, u32[]{:S(2)}) collective-permute-start(f32[1024,256]{1,0:T(8,128)S(1)} %get-tuple-element.23), channel_id=1, source_target_pairs={{0,1},{1,0},{2,3},{3,2},{4,5},{5,4},{6,7},{7,6},{8,9},{9,8},{10,11... | collective-permute-start | bytes 3145736 | tf_op jit(solution)/shard_map/ppermute | solution.py:350
  55.7 0.7 copy-start.1
  71.5 29.6 %collective-permute-start.5 = (bf16[2048,256]{1,0:T(8,128)(2,1)}, bf16[2048,256]{1,0:T(8,128)(2,1)S(1)}, u32[]{:S(2)}, u32[]{:S(2)}) collective-permute-start(bf16[2048,256]{1,0:T(8,128)(2,1)} %get-tuple-element.26), channel_id=1, source_target_pairs={{0,1},{1,0},{2,3},{3,2},{4,5},{5,4},{6,7},{7,6},{8,9},{9,8},{10,11... | collective-permute-start | bytes 3145736 | tf_op jit(solution)/shard_map/ppermute | solution.py:350
  101.1 1.0 copy-start

commit v3 on v2

--- a/solution.py
+++ b/solution.py
@@ -19,6 +19,7 @@
 PAIR = 8
 LIGHT = pl.CostEstimate(flops=0, transcendentals=0, bytes_accessed=0)
 EARLY_VMEM = 56 << 20
+LATE_STEPS = 4
 
 
 def tdot(left, right):
@@ -33,8 +34,12 @@
     return high, mid, low
 
 
-def gram_kernel(x_ref, g_ref, sym_ref, off_ref):
+def gram_kernel(first, x_ref, g_ref, copy_ref, sym_ref, off_ref):
     step = pl.program_id(0)
+
+    @pl.when(step == 0)
+    def _():
+        copy_ref[...] = x_ref[first:first + copy_ref.shape[0], :]
 
     @pl.when(step == 0)
     def _():
@@ -52,14 +57,20 @@
         g_ref[...] = sym_ref[...] + (off + off.T)
 
 
-def local_gram(snapshots):
+def local_gram(snapshots, first, stop):
     rows, width = snapshots.shape
     return pl.pallas_call(
-        gram_kernel,
+        functools.partial(gram_kernel, first),
         grid=(rows // GRAM_TILE,),
         in_specs=[pl.BlockSpec((GRAM_TILE, width), lambda i: (i, 0))],
-        out_specs=pl.BlockSpec((width, width), lambda i: (0, 0)),
-        out_shape=jax.ShapeDtypeStruct((width, width), jnp.float32),
+        out_specs=[
+            pl.BlockSpec((width, width), lambda i: (0, 0)),
+            pl.BlockSpec((stop - first, width), lambda i: (0, 0)),
+        ],
+        out_shape=[
+            jax.ShapeDtypeStruct((width, width), jnp.float32),
+            jax.ShapeDtypeStruct((stop - first, width), jnp.float32),
+        ],
         scratch_shapes=[pltpu.VMEM((width, width), jnp.float32)] * 2,
         cost_estimate=LIGHT,
         name="local_gram",
@@ -159,13 +170,7 @@
     return jnp.dot(terms, inverse, preferred_element_type=jnp.float32)
 
 
-def own_basis_kernel(x_ref, inv_ref, *refs):
-    half_ref, turned_ref = refs[-2:]
-    basis = basis_of(x_ref[...], inv_ref[...])
-    half = basis.astype(jnp.bfloat16)
-    half_ref[...] = half
-    if len(refs) == 3:
-        refs[0][...] = half
+def turn(basis, turned_ref):
     turned = basis.T
     high = turned.astype(jnp.bfloat16)
     rest = (turned - high.astype(jnp.float32)).astype(jnp.bfloat16)
@@ -175,54 +180,87 @@
         turned_ref[i] = jnp.concatenate([high[:, span], rest[:, span]], axis=1)
 
 
-def own_basis(snapshots, inverse, start, stop, size, held=None):
+def late_basis_kernel(x_ref, inv_ref, send_ref, half_ref, turned_ref):
+    basis = basis_of(x_ref[...], inv_ref[...])
+    half = basis.astype(jnp.bfloat16)
+    send_ref[...] = half
+    half_ref[...] = half
+    turn(basis, turned_ref)
+
+
+def late_basis(snapshots, inverse, start, size):
     rows, width = snapshots.shape
-    tile = math.gcd(math.gcd(start, stop), ROW_TILE)
+    tile = math.gcd(math.gcd(start, rows), ROW_TILE)
     first = start // tile
     shifted = pl.BlockSpec((tile, width), lambda i: (i + first, 0))
-    half = jax.ShapeDtypeStruct((rows, width), jnp.bfloat16)
-    turned = jax.ShapeDtypeStruct((rows // size, width, 2 * size), jnp.bfloat16)
-    out_specs = [shifted, pl.BlockSpec((tile // size, width, 2 * size), lambda i: (i + first, 0, 0))]
-    out_shape = [half, turned]
-    if held is None:
-        out_specs = [pl.BlockSpec((tile, width), lambda i: (i, 0))] + out_specs
-        out_shape = [jax.ShapeDtypeStruct((stop - start, width), jnp.bfloat16)] + out_shape
-    held = held or []
-    return pl.pallas_call(
-        own_basis_kernel,
-        grid=((stop - start) // tile,),
-        in_specs=[shifted, pl.BlockSpec(inverse.shape, lambda i: (0, 0))]
-        + [pl.BlockSpec(memory_space=pl.ANY)] * len(held),
-        out_specs=out_specs,
-        out_shape=out_shape,
-        input_output_aliases={2 + i: i for i in range(len(held))},
-        cost_estimate=LIGHT,
-        name="own_basis",
-    )(snapshots, inverse, *held)
-
-
-def other_basis_kernel(switch, one_ref, two_ref, inv_ref, out_ref):
-    value = jnp.where(pl.program_id(0) < switch, one_ref[...], two_ref[...])
-    out_ref[...] = basis_of(value, inv_ref[...]).astype(jnp.bfloat16)
-
-
-def other_basis(one, two, inverse):
-    width = one.shape[1]
+    return pl.pallas_call(
+        late_basis_kernel,
+        grid=((rows - start) // tile,),
+        in_specs=[shifted, pl.BlockSpec(inverse.shape, lambda i: (0, 0))],
+        out_specs=[
+            pl.BlockSpec((tile, width), lambda i: (i, 0)),
+            shifted,
+            pl.BlockSpec((tile // size, width, 2 * size), lambda i: (i + first, 0, 0)),
+        ],
+        out_shape=[
+            jax.ShapeDtypeStruct((rows - start, width), jnp.bfloat16),
+            jax.ShapeDtypeStruct((rows, width), jnp.bfloat16),
+            jax.ShapeDtypeStruct((rows // size, width, 2 * size), jnp.bfloat16),
+        ],
+        compiler_params=pltpu.CompilerParams(vmem_limit_bytes=EARLY_VMEM),
+        cost_estimate=LIGHT,
+        name="late_basis",
+    )(snapshots, inverse)
+
+
+def early_basis_kernel(ends, x_ref, one_ref, two_ref, inv_ref, _, __, half_ref, turned_ref, other_ref):
+    step = pl.program_id(0)
+    value = jnp.where(step < ends[0], x_ref[...], jnp.where(step < ends[1], one_ref[...], two_ref[...]))
+    basis = basis_of(value, inv_ref[...])
+
+    @pl.when(step < ends[0])
+    def _():
+        half_ref[...] = basis.astype(jnp.bfloat16)
+        turn(basis, turned_ref)
+
+    @pl.when(step >= ends[0])
+    def _():
+        other_ref[...] = basis.astype(jnp.bfloat16)
+
+
+def early_basis(snapshots, one, two, inverse, half, turned):
+    width = snapshots.shape[1]
     tile = math.gcd(math.gcd(one.shape[0], two.shape[0]), ROW_TILE)
-    switch, steps = one.shape[0] // tile, (one.shape[0] + two.shape[0]) // tile
-    return pl.pallas_call(
-        functools.partial(other_basis_kernel, switch),
-        grid=(steps,),
+    own = (one.shape[0] + two.shape[0]) // tile
+    mid = own + one.shape[0] // tile
+    spec = lambda index: pl.BlockSpec((tile, width), index)
+    here = lambda i: jnp.minimum(i, own - 1)
+    return pl.pallas_call(
+        functools.partial(early_basis_kernel, (own, mid)),
+        grid=(2 * own,),
         in_specs=[
-            pl.BlockSpec((tile, width), lambda i: (jnp.minimum(i, switch - 1), 0)),
-            pl.BlockSpec((tile, width), lambda i: (jnp.maximum(i - switch, 0), 0)),
+            spec(lambda i: (here(i), 0)),
+            spec(lambda i: (jnp.clip(i - own, 0, mid - own - 1), 0)),
+            spec(lambda i: (jnp.maximum(i - mid, 0), 0)),
             pl.BlockSpec(inverse.shape, lambda i: (0, 0)),
-        ],
-        out_specs=pl.BlockSpec((tile, width), lambda i: (i, 0)),
-        out_shape=jax.ShapeDtypeStruct((steps * tile, width), jnp.bfloat16),
-        cost_estimate=LIGHT,
-        name="other_basis",
-    )(one, two, inverse)
+            pl.BlockSpec(memory_space=pl.ANY),
+            pl.BlockSpec(memory_space=pl.ANY),
+        ],
+        out_specs=[
+            spec(lambda i: (here(i), 0)),
+            pl.BlockSpec((tile * turned.shape[0] // snapshots.shape[0],) + turned.shape[1:], lambda i: (here(i), 0, 0)),
+            spec(lambda i: (jnp.maximum(i - own, 0), 0)),
+        ],
+        out_shape=[
+            jax.ShapeDtypeStruct(half.shape, half.dtype),
+            jax.ShapeDtypeStruct(turned.shape, turned.dtype),
+            jax.ShapeDtypeStruct((own * tile, width), half.dtype),
+        ],
+        input_output_aliases={4: 0, 5: 1},
+        compiler_params=pltpu.CompilerParams(vmem_limit_bytes=EARLY_VMEM),
+        cost_estimate=LIGHT,
+        name="early_basis",
+    )(snapshots, one, two, inverse, half, turned)
 
 
 def split_pair(value):
@@ -310,22 +348,33 @@
 
 
 def late_kernel(early_ref, left_ref, half_ref, out_ref):
-    total = early_ref[...]
+    @pl.when(pl.program_id(0) == 0)
+    def _():
+        out_ref[...] = early_ref[...]
+
+    total = out_ref[...]
     for c in range(left_ref.shape[0]):
         total += jnp.dot(left_ref[c], doubled(half_ref[c]), preferred_element_type=jnp.float32)
     out_ref[...] = total
 
 
 def late_terms(early, left, half):
-    size = left.shape[2] // 2
+    slots, width, size = left.shape[0], left.shape[1], left.shape[2] // 2
+    step = slots // LATE_STEPS
     return pl.pallas_call(
         late_kernel,
-        in_specs=[pl.BlockSpec(memory_space=pltpu.VMEM)] * 3,
-        out_specs=pl.BlockSpec(memory_space=pltpu.VMEM),
+        grid=(LATE_STEPS,),
+        in_specs=[
+            pl.BlockSpec((width, width), lambda i: (0, 0)),
+            pl.BlockSpec((step, width, 2 * size), lambda i: (i, 0, 0)),
+            pl.BlockSpec((step, size, width), lambda i: (i, 0, 0)),
+        ],
+        out_specs=pl.BlockSpec((width, width), lambda i: (0, 0)),
         out_shape=jax.ShapeDtypeStruct(early.shape, jnp.float32),
+        compiler_params=pltpu.CompilerParams(vmem_limit_bytes=EARLY_VMEM),
         cost_estimate=LIGHT,
         name="late_terms",
-    )(early, left, half.reshape(left.shape[0], size, half.shape[1]))
+    )(early, left, half.reshape(slots, size, width))
 
 
 def spread(value, axes):
@@ -356,19 +405,19 @@
     count = rows // size
     first, raw = FIRST * size, RAW * size
     partner_first = exchange(snapshots[:first], "yl", 1)
-    share = reduce_share(local_gram(snapshots), SIDE)
+    gram, following = local_gram(snapshots, first, raw)
+    share = reduce_share(gram, SIDE)
     share, partner_first = lax.optimization_barrier((share, partner_first))
     near = [exchange(share, ("yh", "yl"), mask) for mask in (1, 2, 3)]
     share = (share + near[0]) + (near[1] + near[2])
-    share, following = lax.optimization_barrier((share, snapshots[first:raw]))
+    share, following = lax.optimization_barrier((share, following))
     partner_second = exchange(following, "yl", 1)
     gram = spread(share, SIDE)
     total_rows = rows * lax.axis_size(AXES)
     scaled_factor, inverse = factorize(gram, 1.0 / math.sqrt(total_rows))
-    late_half, half, turned = own_basis(snapshots, inverse, raw, rows, size)
+    late_half, half, turned = late_basis(snapshots, inverse, raw, size)
     partner_late = exchange(late_half, "yl", 1)
-    half, turned = own_basis(snapshots, inverse, 0, raw, size, [half, turned])
-    other_half = other_basis(partner_first, partner_second, inverse)
+    half, turned, other_half = early_basis(snapshots, partner_first, partner_second, inverse, half, turned)
     own = columns // count == lax.axis_index("yl")
     spots = columns % count + jnp.where(own, 0, count)
     early, left = early_terms(spots, blocks, turned, [half, other_half], 2 * count)

time: 140 us -> 143 us (1.021)
  blocking collectives: 49.8 us -> 52.2 us
    all_to_all x2, blocking collectives: 34.5 us -> 36.9 us  [reduce_share(): lax.all_to_all(value.reshape(devices, rows // devices, width), axes, 0, 0...]
    pallas_call x5 -> x4, Pallas kernels: 22.7 us -> 22.8 us  [the longest x1 8.31 us: early_basis(): pl.pallas_call(functools.partial(early_basis_kernel, (own, mid)), grid=(2...]
  transfers between devices with their start and end apart: 7 -> 7, of which waited for: 3 -> 3; matrix products, arithmetic and copies ran while one was open for 1% -> 1% of each run, Pallas kernels for 35% -> 34%
where the time goes in v3:
time: 143 us; the launch traced here: 142 us
  Pallas kernels  52.5 us (37%)
  blocking collectives  52.2 us (37%)
  starting transfers between devices  17.2 us (12%)
  waiting for transfers between devices  12 us (8%)
  local copies, waits for them, and re-layouts  6.83 us (5%)
    all_to_all x2, blocking collectives, reduce_share(): lax.all_to_all(value.reshape(devices, rows // devices, width), axes, 0, 0...  36.9 us
    pallas_call x1, Pallas kernels, early_terms(): pl.pallas_call(functools.partial(early_kernel, places), grid_spec=pltpu.P...  19.6 us
    all_to_all x1, blocking collectives, spread(): lax.all_to_all(copies, axes, 0, 0, tiled=True)  15.2 us
    all_to_all x1, starting transfers between devices, spread(): lax.all_to_all(copies, axes, 0, 0, tiled=True)  10.9 us
    pallas_call x1, Pallas kernels, factorize(): pl.pallas_call(functools.partial(factor_kernel, scale), out_shape=[jax.Sh...  10.1 us
    all_to_all x1, waiting for transfers between devices, spread(): lax.all_to_all(copies, axes, 0, 0, tiled=True)  8.9 us
    pallas_call x1, Pallas kernels, early_basis(): pl.pallas_call(functools.partial(early_basis_kernel, (own, mid)), grid=(2...  8.31 us
    ppermute x6, starting transfers between devices, exchange(): lax.ppermute(value, axes, [(i, i ^ mask) for i in range(lax.axis_size(axe...  6.23 us
  transfers between devices with their start and end apart: 7, of which 3 were waited for; matrix products, arithmetic and copies ran while one was open for 1% of the time, Pallas kernels for 34%

profile of v3, /device:TPU:1, one launch (start us, length us, event | category | flops | bytes accessed | tf_op | source)
XLA Modules:
  0.0 142.2 jit_solution(15641034916382786800)
XLA Ops:
  0.6 1.3 slice.3
  1.9 2.2 %collective-permute-start = (f32[1024,256]{1,0:T(8,128)S(1)}, f32[1024,256]{1,0:T(8,128)S(1)}, u32[]{:S(2)}, u32[]{:S(2)}) collective-permute-start(f32[1024,256]{1,0:T(8,128)S(1)} %slice.3), channel_id=1, source_target_pairs={{0,1},{1,0},{2,3},{3,2},{4,5},{5,4},{6,7},{7,6},{8,9},{9,8},{10,11... | collective-permute-start | bytes 3145736 | tf_op jit(solution)/shard_map/ppermute | solution.py:399
  4.1 5.5 %local_gram.1 = (f32[256,256]{1,0:T(8,128)}, f32[1024,256]{1,0:T(8,128)}) custom-call(f32[4096,256]{1,0:T(8,128)} %x_ref.5), custom_call_target="tpu_custom_call" | custom-call | tf_op jit(solution)/shard_map/local_gram/pallas_call | solution.py:62
  9.7 18.0 %all_to_all.20 = f32[32,8,256]{2,1,0:T(8,128)S(1)} all-to-all(f32[32,8,256]{2,1,0:T(8,128)} %bitcast.9), channel_id=1, replica_groups=mesh['x'=4,'yh'=2,'z'=4,'core'=2,'yl'=2] {'x','z','core'}, dimensions={0} | all-to-all | bytes 524288 | tf_op jit(solution)/shard_map/all_to_all | solution.py:390
  28.2 2.7 %collective-permute-start.2 = (f32[8,256]{1,0:T(8,128)S(1)}, f32[8,256]{1,0:T(8,128)S(1)}, u32[]{:S(2)}, u32[]{:S(2)}) collective-permute-start(f32[8,256]{1,0:T(8,128)S(1)} %reduce_sum.18), channel_id=1, source_target_pairs={{0,16},{1,17},{16,0},{17,1},{2,18},{3,19},{18,2},{19,3},{4,20},{5,... | collective-permute-start | bytes 24584 | tf_op jit(solution)/shard_map/ppermute | solution.py:399
  30.9 0.8 collective-permute-start.3
  31.7 0.5 collective-permute-done.2
  32.2 2.6 %collective-permute-done.3 = f32[8,256]{1,0:T(8,128)S(1)} collective-permute-done((f32[8,256]{1,0:T(8,128)S(1)}, f32[8,256]{1,0:T(8,128)S(1)}, u32[]{:S(2)}, u32[]{:S(2)}) %collective-permute-start.3) | collective-permute-done | bytes 8224 | tf_op jit(solution)/shard_map/ppermute | solution.py:399
  34.8 0.7 broadcast_in_dim.8
  35.5 10.9 %all-to-all-start.1 = ((f32[32,8,256]{2,1,0:T(8,128)}), f32[32,8,256]{2,1,0:T(8,128)S(1)}, u32[]{:S(2)}, u32[]{:S(2)}) async-start(f32[32,8,256]{2,1,0:T(8,128)} %broadcast_in_dim.8), calls=%async_computation.1 | async-start | bytes 524288 | tf_op jit(solution)/shard_map/all_to_all | solution.py:384
  46.5 8.9 %all-to-all-done.1 = f32[32,8,256]{2,1,0:T(8,128)S(1)} async-done(((f32[32,8,256]{2,1,0:T(8,128)}), f32[32,8,256]{2,1,0:T(8,128)S(1)}, u32[]{:S(2)}, u32[]{:S(2)}) %all-to-all-start.1) | async-done | bytes 262176 | tf_op jit(solution)/shard_map/all_to_all | solution.py:384
  55.4 0.7 copy-done.3
  56.1 10.1 %factorize.1 = (f32[256,256]{1,0:T(8,128)}, bf16[1536,256]{1,0:T(8,128)(2,1)}) custom-call(f32[256,256]{1,0:T(8,128)} %bitcast.8), custom_call_target="tpu_custom_call" | custom-call | tf_op jit(solution)/shard_map/factorize/pallas_call | solution.py:153
  66.2 4.9 %late_basis.1 = (bf16[2048,256]{1,0:T(8,128)(2,1)}, bf16[4096,256]{1,0:T(8,128)(2,1)}, bf16[32,256,256]{2,1,0:T(8,128)(2,1)}) custom-call(f32[4096,256]{1,0:T(8,128)} %x_ref.5, bf16[1536,256]{1,0:T(8,128)(2,1)} %get-tuple-element.24.inv_ref), custom_call_target="tpu_custom_call" | custom-call | tf_op jit(solution)/shard_map/late_basis/pallas_call | solution.py:196
  71.2 0.6 fusion.spot_ref
  71.8 1.0 copy-done.2
  72.8 8.3 %early_basis.1 = (bf16[4096,256]{1,0:T(8,128)(2,1)}, bf16[32,256,256]{2,1,0:T(8,128)(2,1)}, bf16[2048,256]{1,0:T(8,128)(2,1)}) custom-call(f32[4096,256]{1,0:T(8,128)} %x_ref.5, f32[1024,256]{1,0:T(8,128)} %copy-done, f32[1024,256]{1,0:T(8,128)} %copy-done.2, ...), custom_call_target="tpu_custom_call", output_to_operand_aliasing={{0}: (4, {}), {1}: (5, {})} | custom-call | tf_op jit(solution)/shard_map/early_basis/pallas_call | solution.py:238
  81.2 19.6 %early_terms.1 = (f32[256,256]{1,0:T(8,128)}, bf16[16,256,256]{2,1,0:T(8,128)(2,1)}) custom-call(s32[32,16]{1,0:T(8,128)} %fusion.spot_ref, bf16[32,16,128,128]{3,2,1,0:T(8,128)(2,1)} %blocks_ref.1, bf16[32,256,256]{2,1,0:T(8,128)(2,1)} %get-tuple-element.27.turned_ref, bf16[32,128,256]{2,1,0:T(8,128)(2,1)} %bitcast.5, bf16[16,128,256]{2,1,0:T(8,128)(2,1)} %bitcast.7), custom_call_target="tpu_custom_call" | custom-call | tf_op jit(solution)/shard_map/early_terms/pallas_call | solution.py:320
  100.8 1.0 copy-done.1
  101.8 4.0 %late_terms.1 = f32[256,256]{1,0:T(8,128)} custom-call(f32[256,256]{1,0:T(8,128)} %get-tuple-element.30.early_ref, bf16[16,256,256]{2,1,0:T(8,128)(2,1)} %get-tuple-element.31.left_ref, bf16[16,128,256]{2,1,0:T(8,128)(2,1)} %bitcast.6), custom_call_target="tpu_custom_call" | custom-call | tf_op jit(solution)/shard_map/late_terms/pallas_call | solution.py:364
  105.8 1.1 reshape.32
  106.9 18.9 %all_to_all.21 = f32[128,2,256]{2,1,0:T(2,128)S(1)} all-to-all(f32[128,2,256]{2,1,0:T(2,128)S(1)} %reshape.32), channel_id=1, replica_groups=mesh['x'=4,'yh'=2,'z'=4,'core'=2,'yl'=2] {'x','yh','z','core','yl'}, dimensions={0} | all-to-all | bytes 524288 | tf_op jit(solution)/shard_map/all_to_all | solution.py:390
  126.0 15.2 %all_to_all.22 = f32[128,2,256]{2,1,0:T(2,128)S(1)} all-to-all(f32[128,2,256]{2,1,0:T(2,128)S(1)} %broadcast_in_dim.9), channel_id=1, replica_groups=mesh['x'=4,'yh'=2,'z'=4,'core'=2,'yl'=2] {'x','yh','z','core','yl'}, dimensions={0} | all-to-all | bytes 524288 | tf_op jit(solution)/shard_map/all_to_all | solution.py:384
  141.3 0.9 reshape.33
  (19 shorter events, 0.9 us)
Async XLA Ops:
  1.9 25.8 %collective-permute-start = (f32[1024,256]{1,0:T(8,128)S(1)}, f32[1024,256]{1,0:T(8,128)S(1)}, u32[]{:S(2)}, u32[]{:S(2)}) collective-permute-start(f32[1024,256]{1,0:T(8,128)S(1)} %slice.3), channel_id=1, source_target_pairs={{0,1},{1,0},{2,3},{3,2},{4,5},{5,4},{6,7},{7,6},{8,9},{9,8},{10,11... | collective-permute-start | bytes 3145736 | tf_op jit(solution)/shard_map/ppermute | solution.py:399
  9.7 61.5 %copy-start.4 = (s32[32,16]{0,1:T(8,128)S(1)}, s32[32,16]{0,1:T(8,128)}, u32[]{:S(2)}) copy-start(s32[32,16]{0,1:T(8,128)} %param.5) | copy-start | bytes 6148
  27.7 44.1 %copy-start = (f32[1024,256]{1,0:T(8,128)}, f32[1024,256]{1,0:T(8,128)S(1)}, u32[]{:S(2)}) copy-start(f32[1024,256]{1,0:T(8,128)S(1)} %collective-permute-done.one_ref) | copy-start | bytes 3145732
  27.7 3.9 %collective-permute-start.1 = (f32[8,256]{1,0:T(8,128)S(1)}, f32[8,256]{1,0:T(8,128)S(1)}, u32[]{:S(2)}, u32[]{:S(2)}) collective-permute-start(f32[8,256]{1,0:T(8,128)S(1)} %reduce_sum.18), channel_id=1, source_target_pairs={{0,1},{1,0},{16,17},{17,16},{2,3},{3,2},{18,19},{19,18},{4,5},{5,4... | collective-permute-start | bytes 24584 | tf_op jit(solution)/shard_map/ppermute | solution.py:399
  28.2 4.0 %collective-permute-start.2 = (f32[8,256]{1,0:T(8,128)S(1)}, f32[8,256]{1,0:T(8,128)S(1)}, u32[]{:S(2)}, u32[]{:S(2)}) collective-permute-start(f32[8,256]{1,0:T(8,128)S(1)} %reduce_sum.18), channel_id=1, source_target_pairs={{0,16},{1,17},{16,0},{17,1},{2,18},{3,19},{18,2},{19,3},{4,20},{5,... | collective-permute-start | bytes 24584 | tf_op jit(solution)/shard_map/ppermute | solution.py:399
  30.9 3.9 %collective-permute-start.3 = (f32[8,256]{1,0:T(8,128)S(1)}, f32[8,256]{1,0:T(8,128)S(1)}, u32[]{:S(2)}, u32[]{:S(2)}) collective-permute-start(f32[8,256]{1,0:T(8,128)S(1)} %reduce_sum.18), channel_id=1, source_target_pairs={{0,17},{1,16},{16,1},{17,0},{2,19},{3,18},{18,3},{19,2},{4,21},{5,... | collective-permute-start | bytes 24584 | tf_op jit(solution)/shard_map/ppermute | solution.py:399
  35.5 19.9 %all-to-all-start.1 = ((f32[32,8,256]{2,1,0:T(8,128)}), f32[32,8,256]{2,1,0:T(8,128)S(1)}, u32[]{:S(2)}, u32[]{:S(2)}) async-start(f32[32,8,256]{2,1,0:T(8,128)} %broadcast_in_dim.8), calls=%async_computation.1 | async-start | bytes 524288 | tf_op jit(solution)/shard_map/all_to_all | solution.py:384
  46.4 25.4 %collective-permute-start.4 = (f32[1024,256]{1,0:T(8,128)}, f32[1024,256]{1,0:T(8,128)S(1)}, u32[]{:S(2)}, u32[]{:S(2)}) collective-permute-start(f32[1024,256]{1,0:T(8,128)} %get-tuple-element.22), channel_id=1, source_target_pairs={{0,1},{1,0},{2,3},{3,2},{4,5},{5,4},{6,7},{7,6},{8,9},{9,8},{10,11... | collective-permute-start | bytes 3145736 | tf_op jit(solution)/shard_map/ppermute | solution.py:399
  55.4 0.7 copy-start.3
  71.1 29.6 %collective-permute-start.5 = (bf16[2048,256]{1,0:T(8,128)(2,1)}, bf16[2048,256]{1,0:T(8,128)(2,1)S(1)}, u32[]{:S(2)}, u32[]{:S(2)}) collective-permute-start(bf16[2048,256]{1,0:T(8,128)(2,1)} %get-tuple-element.32), channel_id=1, source_target_pairs={{0,1},{1,0},{2,3},{3,2},{4,5},{5,4},{6,7},{7,6},{8,9},{9,8},{10,11... | collective-permute-start | bytes 3145736 | tf_op jit(solution)/shard_map/ppermute | solution.py:399
  71.8 1.0 copy-start.2
  100.8 1.0 copy-start.1

commit v4 on v2

--- a/solution.py
+++ b/solution.py
@@ -12,8 +12,8 @@
 AXES = ("x", "yh", "z", "core", "yl")
 SIDE = ("x", "z", "core")
 PANEL = 64
-FIRST = 8
-RAW = 16
+FIRST = 4
+RAW = 12
 GRAM_TILE = 2048
 ROW_TILE = 1024
 PAIR = 8
@@ -33,8 +33,12 @@
     return high, mid, low
 
 
-def gram_kernel(x_ref, g_ref, sym_ref, off_ref):
+def gram_kernel(x_ref, g_ref, lead_ref, sym_ref, off_ref):
     step = pl.program_id(0)
+
+    @pl.when(step == 0)
+    def _():
+        lead_ref[...] = x_ref[:lead_ref.shape[0], :]
 
     @pl.when(step == 0)
     def _():
@@ -52,14 +56,15 @@
         g_ref[...] = sym_ref[...] + (off + off.T)
 
 
-def local_gram(snapshots):
+def local_gram(snapshots, first):
     rows, width = snapshots.shape
+    shapes = [(width, width), (first, width)]
     return pl.pallas_call(
         gram_kernel,
         grid=(rows // GRAM_TILE,),
         in_specs=[pl.BlockSpec((GRAM_TILE, width), lambda i: (i, 0))],
-        out_specs=pl.BlockSpec((width, width), lambda i: (0, 0)),
-        out_shape=jax.ShapeDtypeStruct((width, width), jnp.float32),
+        out_specs=[pl.BlockSpec(shape, lambda i: (0, 0)) for shape in shapes],
+        out_shape=[jax.ShapeDtypeStruct(shape, jnp.float32) for shape in shapes],
         scratch_shapes=[pltpu.VMEM((width, width), jnp.float32)] * 2,
         cost_estimate=LIGHT,
         name="local_gram",
@@ -355,8 +360,9 @@
     size = blocks.shape[2]
     count = rows // size
     first, raw = FIRST * size, RAW * size
-    partner_first = exchange(snapshots[:first], "yl", 1)
-    share = reduce_share(local_gram(snapshots), SIDE)
+    gram, leading = local_gram(snapshots, first)
+    partner_first = exchange(leading, "yl", 1)
+    share = reduce_share(gram, SIDE)
     share, partner_first = lax.optimization_barrier((share, partner_first))
     near = [exchange(share, ("yh", "yl"), mask) for mask in (1, 2, 3)]
     share = (share + near[0]) + (near[1] + near[2])
@@ -366,6 +372,7 @@
     total_rows = rows * lax.axis_size(AXES)
     scaled_factor, inverse = factorize(gram, 1.0 / math.sqrt(total_rows))
     late_half, half, turned = own_basis(snapshots, inverse, raw, rows, size)
+    late_half, partner_second = lax.optimization_barrier((late_half, partner_second))
     partner_late = exchange(late_half, "yl", 1)
     half, turned = own_basis(snapshots, inverse, 0, raw, size, [half, turned])
     other_half = other_basis(partner_first, partner_second, inverse)

time: 140 us -> 135 us (0.964)
  blocking collectives: 49.8 us -> 63.3 us
  waiting for transfers between devices: 12.1 us -> 1.63 us
  starting transfers between devices: 16.4 us -> 8.07 us
  local copies, waits for them, and re-layouts: 7.17 us -> 4.52 us
  Pallas kernels: 52.4 us -> 55 us
    all_to_all x1 -> x2, blocking collectives: 15.2 us -> 29.9 us  [spread(): lax.all_to_all(copies, axes, 0, 0, tiled=True)]
    all_to_all x1 -> x0, starting transfers between devices: 10.9 us -> none  [spread(): lax.all_to_all(copies, axes, 0, 0, tiled=True)]
    all_to_all x1 -> x0, waiting for transfers between devices: 8.89 us -> none  [spread(): lax.all_to_all(copies, axes, 0, 0, tiled=True)]
    ppermute x6, starting transfers between devices: 5.55 us -> 8.07 us  [exchange(): lax.ppermute(value, axes, [(i, i ^ mask) for i in range(lax.axis_size(axe...]
    pallas_call x2, Pallas kernels: 9.69 us -> 11.6 us  [own_basis(): pl.pallas_call(own_basis_kernel, grid=((stop - start) // tile,), in_specs...]
    ppermute x6, waiting for transfers between devices: 3.25 us -> 1.63 us  [exchange(): lax.ppermute(value, axes, [(i, i ^ mask) for i in range(lax.axis_size(axe...]
  transfers between devices with their start and end apart: 7 -> 6, of which waited for: 3 -> 1; matrix products, arithmetic and copies ran while one was open for 1% -> 2% of each run, Pallas kernels for 35% -> 34%
where the time goes in v4:
time: 135 us; the launch traced here: 134 us
  blocking collectives  63.3 us (47%)
  Pallas kernels  55 us (41%)
  starting transfers between devices  8.07 us (6%)
  local copies, waits for them, and re-layouts  4.52 us (3%)
  waiting for transfers between devices  1.63 us (1%)
    all_to_all x2, blocking collectives, reduce_share(): lax.all_to_all(value.reshape(devices, rows // devices, width), axes, 0, 0...  33.5 us
    all_to_all x2, blocking collectives, spread(): lax.all_to_all(copies, axes, 0, 0, tiled=True)  29.9 us
    pallas_call x1, Pallas kernels, early_terms(): pl.pallas_call(functools.partial(early_kernel, places), grid_spec=pltpu.P...  19.7 us
    pallas_call x2, Pallas kernels, own_basis(): pl.pallas_call(own_basis_kernel, grid=((stop - start) // tile,), in_specs...  11.6 us
    pallas_call x1, Pallas kernels, factorize(): pl.pallas_call(functools.partial(factor_kernel, scale), out_shape=[jax.Sh...  10.1 us
    ppermute x6, starting transfers between devices, exchange(): lax.ppermute(value, axes, [(i, i ^ mask) for i in range(lax.axis_size(axe...  8.07 us
    pallas_call x1, Pallas kernels, local_gram(): pl.pallas_call(gram_kernel, grid=(rows // GRAM_TILE,), in_specs=[pl.Block...  5.28 us
    pallas_call x1, Pallas kernels, other_basis(): pl.pallas_call(functools.partial(other_basis_kernel, switch), grid=(steps...  4.5 us
  transfers between devices with their start and end apart: 6, of which 1 were waited for; matrix products, arithmetic and copies ran while one was open for 2% of the time, Pallas kernels for 34%

profile of v4, /device:TPU:1, one launch (start us, length us, event | category | flops | bytes accessed | tf_op | source)
XLA Modules:
  0.0 134.0 jit_solution(14024745868078611283)
XLA Ops:
  0.6 5.3 %local_gram.1 = (f32[256,256]{1,0:T(8,128)}, f32[512,256]{1,0:T(8,128)}) custom-call(f32[4096,256]{1,0:T(8,128)} %x_ref.5), custom_call_target="tpu_custom_call" | custom-call | tf_op jit(solution)/shard_map/local_gram/pallas_call | solution.py:62
  5.9 2.1 %collective-permute-start = (f32[512,256]{1,0:T(8,128)}, f32[512,256]{1,0:T(8,128)S(1)}, u32[]{:S(2)}, u32[]{:S(2)}) collective-permute-start(f32[512,256]{1,0:T(8,128)} %get-tuple-element.20), channel_id=1, source_target_pairs={{0,1},{1,0},{2,3},{3,2},{4,5},{5,4},{6,7},{7,6},{8,9},{9,8},{10,11... | collective-permute-start | bytes 1572872 | tf_op jit(solution)/shard_map/ppermute | solution.py:355
  8.0 17.9 %all_to_all.20 = f32[32,8,256]{2,1,0:T(8,128)S(1)} all-to-all(f32[32,8,256]{2,1,0:T(8,128)} %bitcast.9), channel_id=1, replica_groups=mesh['x'=4,'yh'=2,'z'=4,'core'=2,'yl'=2] {'x','z','core'}, dimensions={0} | all-to-all | bytes 524288 | tf_op jit(solution)/shard_map/all_to_all | solution.py:346
  26.0 0.3 collective-permute-start.1
  26.2 2.9 %collective-permute-start.2 = (f32[8,256]{1,0:T(8,128)S(1)}, f32[8,256]{1,0:T(8,128)S(1)}, u32[]{:S(2)}, u32[]{:S(2)}) collective-permute-start(f32[8,256]{1,0:T(8,128)S(1)} %reduce_sum.18), channel_id=1, source_target_pairs={{0,16},{1,17},{16,0},{17,1},{2,18},{3,19},{18,2},{19,3},{4,20},{5,... | collective-permute-start | bytes 24584 | tf_op jit(solution)/shard_map/ppermute | solution.py:355
  29.1 0.8 collective-permute-start.3
  29.9 1.3 slice.3
  31.2 1.6 %collective-permute-done.3 = f32[8,256]{1,0:T(8,128)S(1)} collective-permute-done((f32[8,256]{1,0:T(8,128)S(1)}, f32[8,256]{1,0:T(8,128)S(1)}, u32[]{:S(2)}, u32[]{:S(2)}) %collective-permute-start.3) | collective-permute-done | bytes 8224 | tf_op jit(solution)/shard_map/ppermute | solution.py:355
  32.9 14.6 %all_to_all.21 = f32[32,8,256]{2,1,0:T(8,128)} all-to-all(f32[32,8,256]{2,1,0:T(8,128)S(1)} %broadcast_in_dim.8), channel_id=1, replica_groups=mesh['x'=4,'yh'=2,'z'=4,'core'=2,'yl'=2] {'x','z','core'}, dimensions={0} | all-to-all | bytes 524288 | tf_op jit(solution)/shard_map/all_to_all | solution.py:340
  47.5 10.1 %factorize.1 = (f32[256,256]{1,0:T(8,128)}, bf16[1536,256]{1,0:T(8,128)(2,1)}) custom-call(f32[256,256]{1,0:T(8,128)} %bitcast.8), custom_call_target="tpu_custom_call" | custom-call | tf_op jit(solution)/shard_map/factorize/pallas_call | solution.py:147
  57.6 6.9 %own_basis.2 = (bf16[2560,256]{1,0:T(8,128)(2,1)}, bf16[4096,256]{1,0:T(8,128)(2,1)}, bf16[32,256,256]{2,1,0:T(8,128)(2,1)}) custom-call(f32[4096,256]{1,0:T(8,128)} %x_ref.5, bf16[1536,256]{1,0:T(8,128)(2,1)} %get-tuple-element.23.inv_ref), custom_call_target="tpu_custom_call" | custom-call | tf_op jit(solution)/shard_map/own_basis/pallas_call | solution.py:196
  64.6 2.0 %collective-permute-start.5 = (bf16[2560,256]{1,0:T(8,128)(2,1)}, bf16[2560,256]{1,0:T(8,128)(2,1)S(1)}, u32[]{:S(2)}, u32[]{:S(2)}) collective-permute-start(bf16[2560,256]{1,0:T(8,128)(2,1)} %get-tuple-element.34), channel_id=1, source_target_pairs={{0,1},{1,0},{2,3},{3,2},{4,5},{5,4},{6,7},{7,6},{8,9},{9,8},{10,11... | collective-permute-start | bytes 3932168 | tf_op jit(solution)/shard_map/ppermute | solution.py:355
  66.6 0.1 copy.7
  66.6 0.6 fusion.spot_ref
  67.3 4.7 %own_basis.3 = (bf16[4096,256]{1,0:T(8,128)(2,1)}, bf16[32,256,256]{2,1,0:T(8,128)(2,1)}) custom-call(f32[4096,256]{1,0:T(8,128)} %x_ref.5, bf16[1536,256]{1,0:T(8,128)(2,1)} %get-tuple-element.23.inv_ref, bf16[4096,256]{1,0:T(8,128)(2,1)} %get-tuple-element.24.refs_0_, ...), custom_call_target="tpu_custom_call", output_to_operand_aliasing={{0}: (2, {}), {1}: (3, {})} | custom-call | tf_op jit(solution)/shard_map/own_basis/pallas_call | solution.py:196
  72.0 4.5 %other_basis.1 = bf16[1536,256]{1,0:T(8,128)(2,1)} custom-call(f32[512,256]{1,0:T(8,128)} %copy-done.2, f32[1024,256]{1,0:T(8,128)} %copy-done.1, bf16[1536,256]{1,0:T(8,128)(2,1)} %get-tuple-element.23.inv_ref), custom_call_target="tpu_custom_call" | custom-call | tf_op jit(solution)/shard_map/other_basis/pallas_call | solution.py:218
  76.5 19.7 %early_terms.1 = (f32[256,256]{1,0:T(8,128)}, bf16[20,256,256]{2,1,0:T(8,128)(2,1)}) custom-call(s32[32,16]{1,0:T(8,128)} %fusion.spot_ref, bf16[32,16,128,128]{3,2,1,0:T(8,128)(2,1)} %blocks_ref.1, bf16[32,256,256]{2,1,0:T(8,128)(2,1)} %get-tuple-element.26.turned_ref, bf16[32,128,256]{2,1,0:T(8,128)(2,1)} %bitcast.5, bf16[12,128,256]{2,1,0:T(8,128)(2,1)} %bitcast.6), custom_call_target="tpu_custom_call" | custom-call | tf_op jit(solution)/shard_map/early_terms/pallas_call | solution.py:287
  96.2 1.1 copy-done
  97.3 3.7 %late_terms.1 = f32[256,256]{1,0:T(8,128)} custom-call(f32[256,256]{1,0:T(8,128)} %get-tuple-element.32.early_ref, bf16[20,256,256]{2,1,0:T(8,128)(2,1)} %get-tuple-element.33.left_ref, bf16[20,128,256]{2,1,0:T(8,128)(2,1)} %bitcast.7), custom_call_target="tpu_custom_call" | custom-call | tf_op jit(solution)/shard_map/late_terms/pallas_call | solution.py:326
  101.0 1.1 reshape.32
  102.1 15.6 %all_to_all.22 = f32[128,2,256]{2,1,0:T(2,128)S(1)} all-to-all(f32[128,2,256]{2,1,0:T(2,128)S(1)} %reshape.32), channel_id=1, replica_groups=mesh['x'=4,'yh'=2,'z'=4,'core'=2,'yl'=2] {'x','yh','z','core','yl'}, dimensions={0} | all-to-all | bytes 524288 | tf_op jit(solution)/shard_map/all_to_all | solution.py:346
  117.7 0.1 reduce_sum.19
  117.9 15.2 %all_to_all.23 = f32[128,2,256]{2,1,0:T(2,128)S(1)} all-to-all(f32[128,2,256]{2,1,0:T(2,128)S(1)} %broadcast_in_dim.9), channel_id=1, replica_groups=mesh['x'=4,'yh'=2,'z'=4,'core'=2,'yl'=2] {'x','yh','z','core','yl'}, dimensions={0} | all-to-all | bytes 524288 | tf_op jit(solution)/shard_map/all_to_all | solution.py:340
  133.2 0.9 reshape.33
  (17 shorter events, 0.2 us)
Async XLA Ops:
  5.9 20.0 %collective-permute-start = (f32[512,256]{1,0:T(8,128)}, f32[512,256]{1,0:T(8,128)S(1)}, u32[]{:S(2)}, u32[]{:S(2)}) collective-permute-start(f32[512,256]{1,0:T(8,128)} %get-tuple-element.20), channel_id=1, source_target_pairs={{0,1},{1,0},{2,3},{3,2},{4,5},{5,4},{6,7},{7,6},{8,9},{9,8},{10,11... | collective-permute-start | bytes 1572872 | tf_op jit(solution)/shard_map/ppermute | solution.py:355
  26.0 38.6 %copy-start.2 = (f32[512,256]{1,0:T(8,128)}, f32[512,256]{1,0:T(8,128)S(1)}, u32[]{:S(2)}) copy-start(f32[512,256]{1,0:T(8,128)S(1)} %collective-permute-done.one_ref) | copy-start | bytes 1572868
  26.0 5.2 %collective-permute-start.1 = (f32[8,256]{1,0:T(8,128)S(1)}, f32[8,256]{1,0:T(8,128)S(1)}, u32[]{:S(2)}, u32[]{:S(2)}) collective-permute-start(f32[8,256]{1,0:T(8,128)S(1)} %reduce_sum.18), channel_id=1, source_target_pairs={{0,1},{1,0},{16,17},{17,16},{2,3},{3,2},{18,19},{19,18},{4,5},{5,4... | collective-permute-start | bytes 24584 | tf_op jit(solution)/shard_map/ppermute | solution.py:355
  26.2 5.0 %collective-permute-start.2 = (f32[8,256]{1,0:T(8,128)S(1)}, f32[8,256]{1,0:T(8,128)S(1)}, u32[]{:S(2)}, u32[]{:S(2)}) collective-permute-start(f32[8,256]{1,0:T(8,128)S(1)} %reduce_sum.18), channel_id=1, source_target_pairs={{0,16},{1,17},{16,0},{17,1},{2,18},{3,19},{18,2},{19,3},{4,20},{5,... | collective-permute-start | bytes 24584 | tf_op jit(solution)/shard_map/ppermute | solution.py:355
  29.1 3.7 %collective-permute-start.3 = (f32[8,256]{1,0:T(8,128)S(1)}, f32[8,256]{1,0:T(8,128)S(1)}, u32[]{:S(2)}, u32[]{:S(2)}) collective-permute-start(f32[8,256]{1,0:T(8,128)S(1)} %reduce_sum.18), channel_id=1, source_target_pairs={{0,17},{1,16},{16,1},{17,0},{2,19},{3,18},{18,3},{19,2},{4,21},{5,... | collective-permute-start | bytes 24584 | tf_op jit(solution)/shard_map/ppermute | solution.py:355
  32.8 31.7 %collective-permute-start.4 = (f32[1024,256]{1,0:T(8,128)S(1)}, f32[1024,256]{1,0:T(8,128)S(1)}, u32[]{:S(2)}, u32[]{:S(2)}) collective-permute-start(f32[1024,256]{1,0:T(8,128)S(1)} %slice.3), channel_id=1, source_target_pairs={{0,1},{1,0},{2,3},{3,2},{4,5},{5,4},{6,7},{7,6},{8,9},{9,8},{10,11... | collective-permute-start | bytes 3145736 | tf_op jit(solution)/shard_map/ppermute | solution.py:355
  47.5 19.1 %copy-start.3 = (s32[32,16]{0,1:T(8,128)S(1)}, s32[32,16]{0,1:T(8,128)}, u32[]{:S(2)}) copy-start(s32[32,16]{0,1:T(8,128)} %param.5) | copy-start | bytes 6148
  64.6 7.4 %copy-start.1 = (f32[1024,256]{1,0:T(8,128)}, f32[1024,256]{1,0:T(8,128)S(1)}, u32[]{:S(2)}) copy-start(f32[1024,256]{1,0:T(8,128)S(1)} %collective-permute-done.4.two_ref) | copy-start | bytes 3145732
  64.6 31.6 %collective-permute-start.5 = (bf16[2560,256]{1,0:T(8,128)(2,1)}, bf16[2560,256]{1,0:T(8,128)(2,1)S(1)}, u32[]{:S(2)}, u32[]{:S(2)}) collective-permute-start(bf16[2560,256]{1,0:T(8,128)(2,1)} %get-tuple-element.34), channel_id=1, source_target_pairs={{0,1},{1,0},{2,3},{3,2},{4,5},{5,4},{6,7},{7,6},{8,9},{9,8},{10,11... | collective-permute-start | bytes 3932168 | tf_op jit(solution)/shard_map/ppermute | solution.py:355
  96.2 1.1 copy-start
